TPU v7x, 768 devices: a whole 4x8x12 slice. The times are simulated.
768 devices in a mesh: ctx: 16 (over y_hi, x), ch: 48 (over z, y_lo, core).
Axes of the slice: x: 4, y: 8 (y_hi: 4, y_lo: 2; y = y_hi * 2 + y_lo), z: 12, core: 2. Of those that a mesh axis runs over, the one named last changes fastest.
Arguments:
- tokens_in: bfloat16 [12288, 4096], P('ctx'), may hold values from -6 to 6
- w_in: bfloat16 [4096, 3, 3072], P(None, None, 'ch'), may hold values from -0.09375 to 0.09375
- filter_bank: bfloat16 [24, 16, 256], replicated, may hold values from -0.09375 to 0.09375
- lag_blocks: int32 [24, 32], replicated, may hold values from 0 to 95, as said below
- filter_ids: int32 [24, 32], replicated, may hold values from 0 to 15
- grad_out: bfloat16 [3072, 12288], P('ch', 'ctx'), may hold values from -0.019897461 to 0.019897461
Outputs:
- gated_out: bfloat16 [3072, 12288], P('ch', 'ctx')
- w_grad: float32 [4096, 3, 3072], P('ctx', None, 'ch')
- filter_grad: float32 [24, 16, 256], replicated
Inputs may be any that keep to these rules, and one draw needn't show every extreme that they name: `lag_blocks`: in each group's row the 32 lags are distinct and the first is 0; row 0 lists the lag 96 - 1.
All inputs are finite; a program needn't handle non-finite values.
Results may differ from a plain program's by a relative error of at most 0.0058.
The roundings to bfloat16 on the way count: a program that leaves them out, or rounds other values in their place, can miss the bound.
Values may be sent and summed in bfloat16 or wider, within the bound.
No kernel may reach another device: no remote copies, remote signals or barrier semaphores. Data moves between devices by JAX's collectives and lax.ppermute only.
A program may use at most 64 MiB of HBM per device.

v0:
```python
import jax
import jax.numpy as jnp
from jax import lax
from jax.sharding import PartitionSpec as P

GROUP = 128
BLK = 128


def toeplitz_blocks(filter_taps, lag_list):
    entries, tap_span = filter_taps.shape
    block_width = tap_span // 2
    reverse = filter_taps[:, ::-1]
    tiled_taps = jnp.tile(reverse, (1, block_width))
    window = tiled_taps[:, block_width - 1 : block_width - 1 + block_width * (tap_span - 1)]
    matrices = window.reshape(entries, block_width, tap_span - 1)[:, :, :block_width]
    row_index = lax.broadcasted_iota(jnp.int32, (block_width, block_width), 0)
    col_index = lax.broadcasted_iota(jnp.int32, (block_width, block_width), 1)
    upper = (row_index < col_index)[None, :, :] & (lag_list == 0)[:, None, None]
    return (jnp.where(upper, jnp.zeros_like(matrices), matrices), upper)


def diagonal_sums(grad_mats):
    entries, block_width, _ = grad_mats.shape
    flipped = grad_mats[:, :, ::-1]
    padded = jnp.pad(flipped, ((0, 0), (0, 0), (0, block_width)))
    flattened = padded.reshape(entries, 2 * block_width * block_width)[
        :, : block_width * (2 * block_width - 1)
    ]
    skewed = flattened.reshape(entries, block_width, 2 * block_width - 1)
    diag_sums = jnp.sum(skewed, axis=1)
    return jnp.pad(diag_sums, ((0, 0), (1, 0)))


def local(tokens_in, w_in, filter_bank, lag_blocks, filter_ids, grad_out):
    chan_dev, tok_dev = grad_out.shape
    count_ctx = lax.axis_size("ctx")
    ctx_rank = lax.axis_index("ctx")
    seq_total = tok_dev * count_ctx
    block_count = tok_dev // BLK
    group_index = lax.axis_index("ch") * chan_dev // GROUP
    projected = lax.dot_general(
        w_in, tokens_in, (((0,), (1,)), ((), ())), preferred_element_type=jnp.float32
    ).astype(jnp.bfloat16)
    outer = projected[0].astype(jnp.float32)
    inner = projected[1].astype(jnp.float32)
    values = projected[2].astype(jnp.float32)
    mixed = (inner * values).astype(jnp.bfloat16)
    grad_conv = (grad_out.astype(jnp.float32) * outer).astype(jnp.bfloat16)
    mixed_all, conv_all = (
        lax.all_gather(mixed, "ctx", axis=1, tiled=True),
        lax.all_gather(grad_conv, "ctx", axis=1, tiled=True),
    )
    lag_list = lax.dynamic_index_in_dim(lag_blocks, group_index, 0, keepdims=False)
    id_list = lax.dynamic_index_in_dim(filter_ids, group_index, 0, keepdims=False)
    group_bank = lax.dynamic_index_in_dim(filter_bank, group_index, 0, keepdims=False)
    entries = lag_list.shape[0]
    selector = (id_list[:, None] == jnp.arange(group_bank.shape[0])[None, :]).astype(jnp.bfloat16)
    filter_taps = jnp.dot(selector, group_bank, preferred_element_type=jnp.float32).astype(
        jnp.bfloat16
    )
    matrices, upper = toeplitz_blocks(filter_taps, lag_list)
    my_start = ctx_rank * tok_dev
    earlier = jnp.concatenate([jnp.zeros_like(mixed_all), mixed_all], axis=1)
    later_pad = jnp.concatenate([conv_all, jnp.zeros_like(conv_all)], axis=1)

    def slice_back(start_at):
        return lax.dynamic_slice_in_dim(earlier, start_at, tok_dev, 1)

    def slice_ahead(start_at):
        return lax.dynamic_slice_in_dim(later_pad, start_at, tok_dev, 1)

    windows = jax.vmap(slice_back)(seq_total + my_start - lag_list * BLK).reshape(
        entries, chan_dev, block_count, BLK
    )
    conv_out = jnp.einsum(
        "kcnb,kab->cna", windows, matrices, preferred_element_type=jnp.float32
    ).reshape(chan_dev, tok_dev)
    gated_out = (outer * conv_out).astype(jnp.bfloat16)
    ahead_windows = jax.vmap(slice_ahead)(my_start + lag_list * BLK).reshape(
        entries, chan_dev, block_count, BLK
    )
    grad_mixed = jnp.einsum(
        "kcna,kab->cnb", ahead_windows, matrices, preferred_element_type=jnp.float32
    ).reshape(chan_dev, tok_dev)
    grad_first = grad_out.astype(jnp.float32) * conv_out
    grad_second = grad_mixed * values
    grad_third = grad_mixed * inner
    grad_proj = jnp.stack([grad_first, grad_second, grad_third]).astype(jnp.bfloat16)
    w_grad = lax.psum_scatter(
        lax.dot_general(
            tokens_in, grad_proj, (((0,), (2,)), ((), ())), preferred_element_type=jnp.float32
        ),
        "ctx",
        scatter_dimension=0,
        tiled=True,
    )
    own_conv = grad_conv.reshape(chan_dev, block_count, BLK)
    grad_mats = jnp.einsum("cna,kcnb->kab", own_conv, windows, preferred_element_type=jnp.float32)
    grad_mats = jnp.where(upper, jnp.zeros_like(grad_mats), grad_mats)
    grad_taps = diagonal_sums(grad_mats)
    group_table = jnp.dot(
        selector.astype(jnp.float32).T, grad_taps, precision=lax.Precision.HIGHEST
    )
    placed = (jnp.arange(filter_bank.shape[0]) == group_index).astype(jnp.float32)[
        :, None, None
    ] * group_table[None, :, :]
    filter_grad = lax.psum(placed, ("ctx", "ch"))
    return (gated_out, w_grad, filter_grad)


def solution(mesh):
    placed = (P("ctx", None), P(None, None, "ch"), P(), P(), P(), P("ch", "ctx"))
    return jax.shard_map(
        local,
        mesh=mesh,
        in_specs=placed,
        out_specs=(P("ch", "ctx"), P("ctx", None, "ch"), P()),
        check_vma=False,
    )
```

profile of v0, /device:TPU:1, one launch (start us, length us, event | category | flops | bytes accessed | tf_op | source)
XLA Modules:
  0.0 978.4 jit_solution(3548939335506252297)
XLA Ops:
  8.6 5.0 fusion.18
  20.1 9.0 reshape.109
  32.5 55.7 %all-gather.4.cloned.1.call-done = bf16[64,12288]{1,0:T(8,128)(2,1)} async-done(((bf16[64,768]{1,0:T(8,128)(2,1)}), bf16[64,12288]{1,0:T(8,128)(2,1)}) %all-gather.4.cloned.1.call-update) | async-done | bytes 1572880 | tf_op jit(solution)/shard_map/all_gather | solution.py:52
  88.1 3.2 concatenate.14
  93.4 88.1 %while.3 = (s32[]{:T(128)}, bf16[64,24576]{1,0:T(8,128)(2,1)}, s32[32,2]{0,1:T(2,128)S(1)}, bf16[32,64,768]{2,1,0:T(8,128)(2,1)}, s32[]{:T(128)}) while((s32[]{:T(128)}, bf16[64,24576]{1,0:T(8,128)(2,1)}, s32[32,2]{0,1:T(2,128)S(1)}, bf16[32,64,768]{2,1,0:T(8,128)(2,1)}, s32[]{:T(128)}) %tuple.35), condition=%wide.while_cond.1, body=%wide.while_body.1.sunk | while | flops 2 | bytes 197221 | solution.py:71
  113.2 2.2 bitcast_dynamic-update-slice_fusion.5
  129.7 2.2 bitcast_dynamic-update-slice_fusion.5
  140.7 2.2 bitcast_dynamic-update-slice_fusion.5
  154.5 2.2 bitcast_dynamic-update-slice_fusion.5
  157.2 2.2 bitcast_dynamic-update-slice_fusion.5
  160.0 2.2 bitcast_dynamic-update-slice_fusion.5
  162.8 2.2 bitcast_dynamic-update-slice_fusion.5
  165.5 2.2 bitcast_dynamic-update-slice_fusion.5
  168.3 2.2 bitcast_dynamic-update-slice_fusion.5
  171.1 2.2 bitcast_dynamic-update-slice_fusion.5
  173.8 2.2 bitcast_dynamic-update-slice_fusion.5
  179.3 2.2 bitcast_dynamic-update-slice_fusion.5
  181.5 2.9 fusion.24
  185.6 64.8 %all-gather.6.cloned.1.call-done = bf16[1,64,12288]{2,1,0:T(8,128)(2,1)} async-done(((bf16[1,64,768]{2,1,0:T(8,128)(2,1)}), bf16[1,64,12288]{2,1,0:T(8,128)(2,1)}) %all-gather.6.cloned.1.call-update) | async-done | bytes 1572880 | tf_op jit(solution)/shard_map/all_gather | solution.py:51
  250.5 3.2 concatenate.12
  255.7 92.1 %while.2 = (s32[]{:T(128)}, bf16[64,24576]{1,0:T(8,128)(2,1)}, s32[32,2]{0,1:T(2,128)S(1)}, bf16[32,64,768]{2,1,0:T(8,128)(2,1)}, s32[]{:T(128)}) while((s32[]{:T(128)}, bf16[64,24576]{1,0:T(8,128)(2,1)}, s32[32,2]{0,1:T(2,128)S(1)}, bf16[32,64,768]{2,1,0:T(8,128)(2,1)}, s32[]{:T(128)}) %tuple.38), condition=%wide.while_cond, body=%wide.while_body.sunk | while | flops 2 | bytes 197221 | solution.py:68
  256.3 2.3 bitcast_dynamic-update-slice_fusion.4
  259.2 2.3 bitcast_dynamic-update-slice_fusion.4
  262.1 2.3 bitcast_dynamic-update-slice_fusion.4
  264.9 2.3 bitcast_dynamic-update-slice_fusion.4
  267.8 2.3 bitcast_dynamic-update-slice_fusion.4
  270.7 2.3 bitcast_dynamic-update-slice_fusion.4
  273.6 2.3 bitcast_dynamic-update-slice_fusion.4
  276.4 2.3 bitcast_dynamic-update-slice_fusion.4
  279.3 2.3 bitcast_dynamic-update-slice_fusion.4
  282.2 2.3 bitcast_dynamic-update-slice_fusion.4
  285.1 2.3 bitcast_dynamic-update-slice_fusion.4
  287.9 2.3 bitcast_dynamic-update-slice_fusion.4
  290.8 2.3 bitcast_dynamic-update-slice_fusion.4
  293.7 2.3 bitcast_dynamic-update-slice_fusion.4
  296.6 2.3 bitcast_dynamic-update-slice_fusion.4
  299.5 2.3 bitcast_dynamic-update-slice_fusion.4
  302.3 2.3 bitcast_dynamic-update-slice_fusion.4
  305.2 2.3 bitcast_dynamic-update-slice_fusion.4
  308.1 2.3 bitcast_dynamic-update-slice_fusion.4
  311.0 2.3 bitcast_dynamic-update-slice_fusion.4
  313.8 2.3 bitcast_dynamic-update-slice_fusion.4
  316.7 2.3 bitcast_dynamic-update-slice_fusion.4
  319.6 2.3 bitcast_dynamic-update-slice_fusion.4
  322.5 2.3 bitcast_dynamic-update-slice_fusion.4
  325.3 2.3 bitcast_dynamic-update-slice_fusion.4
  328.2 2.3 bitcast_dynamic-update-slice_fusion.4
  331.1 2.3 bitcast_dynamic-update-slice_fusion.4
  334.0 2.3 bitcast_dynamic-update-slice_fusion.4
  336.9 2.3 bitcast_dynamic-update-slice_fusion.4
  339.8 2.3 bitcast_dynamic-update-slice_fusion.4
  342.7 2.3 bitcast_dynamic-update-slice_fusion.4
  345.6 2.3 bitcast_dynamic-update-slice_fusion.4
  347.9 3.1 fusion.21
  351.0 2.5 and_select_fusion
  354.2 16.5 %rev.7 = f32[32,128,128]{1,2,0:T(8,128)} reverse(f32[32,128,128]{1,2,0:T(8,128)} %and_select_fusion), dimensions={2} | reverse | bytes 4194304 | tf_op jit(solution)/shard_map/rev | solution.py:25
  370.7 2.9 copy.35
  375.7 2.4 copy.42
  378.2 2.2 slice.51
  380.4 9.4 reshape.115
  389.8 2.6 reduce_sum.9
  393.6 5.8 fusion.4
  399.5 465.0 %all-reduce.8.cloned.1.call-done = f32[24,16,256]{2,1,0:T(8,128)} async-done(((f32[24,16,256]{2,1,0:T(8,128)}), f32[24,16,256]{2,1,0:T(8,128)}) %all-reduce.8.cloned.1.call-update) | async-done | bytes 393232 | tf_op jit(solution)/shard_map/psum | solution.py:108
  864.5 105.6 %reduce-scatter.2.cloned.1.call-done = f32[256,3,64]{0,2,1:T(8,128)} async-done(((f32[4096,3,64]{0,2,1:T(8,128)}), f32[256,3,64]{0,2,1:T(8,128)}) %reduce-scatter.2.cloned.1.call-update) | async-done | bytes 196624 | tf_op jit(solution)/shard_map/reduce_scatter | solution.py:90
  (193 shorter events, 102.5 us)
Async XLA Ops:
  7.2 1.4 copy-start
  7.2 6.4 copy-start.3
  7.2 80.9 %all-gather.4.cloned.1.call-start = ((), (), s32[]{:S(2)}) async-start(), calls=%async_computation.1 | async-start | bytes 1671168 | tf_op jit(solution)/shard_map/all_gather | solution.py:52
  14.3 236.2 %all-gather.6.cloned.1.call-start = ((), (), s32[]{:S(2)}) async-start(), calls=%async_computation.4 | async-start | bytes 1671168 | tf_op jit(solution)/shard_map/all_gather | solution.py:51
  91.4 90.2 %copy-start.2 = (bf16[32,128,128]{1,2,0:T(8,128)(2,1)S(1)}, bf16[32,128,128]{1,2,0:T(8,128)(2,1)}, u32[]{:S(2)}) copy-start(bf16[32,128,128]{1,2,0:T(8,128)(2,1)} %copy.34) | copy-start | bytes 3145732
  185.4 679.1 %all-reduce.8.cloned.1.call-start = ((), (), s32[]{:S(2)}) async-start(), calls=%async_computation.3 | async-start | bytes 786432 | tf_op jit(solution)/shard_map/psum | solution.py:108
  347.8 3.1 copy-start.1
  347.9 3.1 copy-start.5
  351.0 2.6 copy-start.4
  393.6 576.5 %reduce-scatter.2.cloned.1.call-start = ((), (), s32[]{:S(2)}) async-start(), calls=%async_computation.2 | async-start | bytes 3342336 | tf_op jit(solution)/shard_map/reduce_scatter | solution.py:90
Sparse Core Ops, SparseCore 0:
  14.4 73.6 all-gather.3
  185.5 64.9 all-gather.5
  393.7 470.7 all-reduce.7
  869.7 100.3 reduce-scatter.1
where the time goes:
time: 983 us; the launch traced here: 978 us
  waiting for transfers between devices  691 us (70%)
  local copies, waits for them, and re-layouts  245 us (25%)
  matrix products  20.5 us (2%)
  between operations  14 us (1%)
    psum x1, waiting for transfers between devices, local(): filter_grad = lax.psum(placed, ('ctx', 'ch'))  465 us
    gather x192, local copies, waits for them, and re-layouts  180 us
    reduce_scatter x1, waiting for transfers between devices, local(): lax.psum_scatter(lax.dot_general(tokens_in, grad_proj, (((0,), (2,)), (()...  106 us
    all_gather x1, waiting for transfers between devices, local(): lax.all_gather(mixed, 'ctx', axis=1, tiled=True)  64.8 us
    all_gather x1, waiting for transfers between devices, local(): lax.all_gather(grad_conv, 'ctx', axis=1, tiled=True)  55.7 us
  transfers between devices with their start and end apart: 4, of which 4 were waited for; matrix products, arithmetic and copies ran while one was open for 2% of the time, Pallas kernels for 0%

commit v1 on v0

v1 whole, which is shorter than its diff:
```python
import jax
import jax.numpy as jnp
from jax import lax
from jax.experimental import pallas as pl
from jax.experimental.pallas import tpu as pltpu
from jax.sharding import PartitionSpec as P

BLK = 128
HALF = 4
BF16, F32 = jnp.bfloat16, jnp.float32


def low_rows(shape):
    return lax.broadcasted_iota(jnp.int32, shape, len(shape) - 2) < HALF


def project_kernel(w_ref, tok_ref, cot_ref, proj_ref, send_ref):
    chan = cot_ref.shape[0]
    width = tok_ref.shape[0]
    proj = lax.dot_general(
        w_ref[...], tok_ref[...], (((1,), (1,)), ((), ())), preferred_element_type=F32
    ).astype(BF16)
    proj_ref[...] = proj
    wide = proj.astype(F32)
    mixed = wide[chan : 2 * chan] * wide[2 * chan :]
    grad_conv = cot_ref[...].astype(F32) * wide[:chan]
    mixed = mixed.reshape(chan // 8, 8, width)
    grad_conv = grad_conv.reshape(chan // 8, 8, width)
    low = low_rows(mixed.shape)
    send_ref[:, 0] = jnp.where(low, mixed, pltpu.roll(grad_conv, HALF, 1)).astype(BF16)
    send_ref[:, 1] = jnp.where(low, pltpu.roll(mixed, HALF, 1), grad_conv).astype(BF16)


def matrices_kernel(group_ref, ids_ref, bank_ref, rhs_ref, bank_f32):
    stored = bank_ref.shape[1]
    bank_f32[...] = bank_ref[0].astype(F32)
    first = ids_ref[group_ref[0], 0]
    row = lax.broadcasted_iota(jnp.int32, (BLK, BLK), 0)
    col = lax.broadcasted_iota(jnp.int32, (BLK, BLK), 1)
    rhs_ref[stored // 2, :, BLK:] = jnp.zeros((2 * BLK, BLK), BF16)
    for f in range(stored + 1):
        taps = bank_f32[pl.ds(first if f == stored else f, 1), :]
        rows = jnp.broadcast_to(taps, (BLK, 2 * BLK))
        turned = pltpu.roll(rows, BLK, 1, stride=1, stride_axis=0)[:, :BLK]
        if f == stored:
            turned = jnp.where(col >= row, turned, 0.0)
        lanes = slice((f % 2) * BLK, (f % 2 + 1) * BLK)
        rhs_ref[f // 2, :BLK, lanes] = turned.astype(BF16)
        rhs_ref[f // 2, BLK:, lanes] = turned.T.astype(BF16)


def convolve_kernel(
    group_ref, lags_ref, ids_ref, x_ref, rhs_ref, out_ref, lhs, prod, res, *scratch
):
    conv_part(group_ref, lags_ref, ids_ref, x_ref, rhs_ref, out_ref, lhs, prod, res)
    filter_part(group_ref, lags_ref, ids_ref, x_ref, out_ref, *scratch)


def conv_part(group_ref, lags_ref, ids_ref, x_ref, rhs_ref, out_ref, lhs, prod, res):
    peers, _, tok = x_ref.shape
    per = tok // BLK
    blocks = peers * per
    pairs = rhs_ref.shape[0]
    stored = 2 * (pairs - 1)
    entries = lags_ref.shape[1]
    group = group_ref[0]
    low = low_rows((8, BLK))
    zero = jnp.zeros((8, BLK), F32)

    def tile(i):
        return x_ref[i // per, :, (i % per) * BLK : (i % per + 1) * BLK].astype(F32)

    for i in range(0, blocks, 2):
        left = [jnp.where(low, tile(i + j), zero) for j in (0, 1)]
        right = [jnp.where(low, zero, tile(blocks - 1 - i - j)) for j in (0, 1)]
        lhs[i * 8 : i * 8 + 16, :BLK] = jnp.concatenate(left, 0).astype(BF16)
        lhs[i * 8 : i * 8 + 16, BLK:] = jnp.concatenate(right, 0).astype(BF16)

    def product(pair, carry):
        both = jnp.dot(lhs[...], rhs_ref[pair], preferred_element_type=F32)
        for j in (0, 1):
            half = both[:, j * BLK : (j + 1) * BLK].reshape(blocks, 8, BLK)
            prod[2 * pair + j, blocks:] = half
            prod[2 * pair + j, :blocks] = jnp.zeros((blocks, 8, BLK), F32)
        return carry

    lax.fori_loop(0, pairs, product, 0)
    chunk = 24
    for start in range(0, blocks, chunk):

        def add(k, acc):
            return acc + prod[ids_ref[group, k], pl.ds(blocks + start - lags_ref[group, k], chunk)]

        acc = prod[stored, blocks + start : blocks + start + chunk]
        res[start : start + chunk] = lax.fori_loop(1, entries, add, acc)
    for i in range(blocks):
        both = jnp.where(low, res[i], res[blocks - 1 - i])
        out_ref[i // per, :, (i % per) * BLK : (i % per + 1) * BLK] = both.astype(BF16)


def filter_part(group_ref, lags_ref, ids_ref, x_ref, out_ref, padded, cots, turned, sums, folded):
    peers, _, tok = x_ref.shape
    per = tok // BLK
    blocks = peers * per
    entries = lags_ref.shape[1]
    stored = sums.shape[0]
    group = group_ref[0]
    low = low_rows((8, BLK))
    padded[:blocks] = jnp.zeros((blocks, 8, BLK), F32)
    for i in range(blocks):
        tile = x_ref[i // per, :, (i % per) * BLK : (i % per + 1) * BLK].astype(F32)
        padded[blocks + i] = jnp.where(low, tile, 0.0)
        cots[i] = jnp.where(low, pltpu.roll(tile, HALF, 0), 0.0)
    step = BLK // 8
    for j in range(blocks // step):
        rows = cots[j * step : (j + 1) * step].reshape(BLK, BLK)
        turned[:, j * BLK : (j + 1) * BLK] = rows.T.astype(BF16)
    sums[...] = jnp.zeros(sums.shape, F32)
    row = lax.broadcasted_iota(jnp.int32, (BLK, BLK), 0)
    col = lax.broadcasted_iota(jnp.int32, (BLK, BLK), 1)

    def pair(p, carry):
        k = 2 * p
        shifted = [padded[pl.ds(blocks - lags_ref[group, k + j], blocks)] for j in (0, 1)]
        shifted = [s.reshape(blocks * 8, BLK).astype(BF16) for s in shifted]
        both = jnp.dot(turned[...], jnp.concatenate(shifted, 1), preferred_element_type=F32)
        keep = (row >= col) | (k > 0)
        sums[ids_ref[group, k]] += jnp.where(keep, both[:, :BLK], 0.0)
        sums[ids_ref[group, k + 1]] += both[:, BLK:]
        return carry

    lax.fori_loop(0, entries // 2, pair, 0)
    for f in range(stored):
        mat = jnp.concatenate([jnp.zeros((BLK, BLK), F32), sums[f].T], 1)
        total = mat[:8]
        for q in range(1, BLK // 8):
            total += pltpu.roll(mat[8 * q : 8 * q + 8], 2 * BLK - 8 * q, 1)
        folded[f] = total
    total = folded[:, 0]
    for s in range(1, 8):
        total += pltpu.roll(folded[:, s], 2 * BLK - s, 1)
    high = total.astype(BF16).astype(F32)
    rest = total - high
    sub = lax.broadcasted_iota(jnp.int32, (8, BLK), 0)
    for p in range(peers):
        piece = jnp.zeros((8, BLK), F32)
        for r, part in enumerate((high[:, :BLK], high[:, BLK:], rest[:, :BLK], rest[:, BLK:])):
            piece = jnp.where(sub == r, part[p : p + 1], piece)
        out_ref[p, :, tok:] = piece.astype(BF16)


def weights_kernel(back_ref, proj_ref, cot_ref, tok_ref, gated_ref, out_ref, grads):
    chan, tok = cot_ref.shape

    @pl.when(pl.program_id(0) == 0)
    def _():
        even = back_ref[:, 0, :, :tok].astype(F32)
        odd = back_ref[:, 1, :, :tok].astype(F32)
        low = low_rows(even.shape)
        conv_out = jnp.where(low, even, pltpu.roll(odd, HALF, 1)).reshape(chan, tok)
        grad_mixed = jnp.where(low, pltpu.roll(even, HALF, 1), odd).reshape(chan, tok)
        gated_ref[...] = (proj_ref[:chan].astype(F32) * conv_out).astype(BF16)
        grads[:chan] = (cot_ref[...].astype(F32) * conv_out).astype(BF16)
        grads[chan : 2 * chan] = (grad_mixed * proj_ref[2 * chan :].astype(F32)).astype(BF16)
        grads[2 * chan :] = (grad_mixed * proj_ref[chan : 2 * chan].astype(F32)).astype(BF16)

    both = jnp.dot(grads[...], tok_ref[...], preferred_element_type=F32)
    share = out_ref.shape[2]
    for j in range(out_ref.shape[0]):
        out_ref[j] = both[:, j * share : (j + 1) * share].astype(out_ref.dtype)


def spread_kernel(back_ref, out_ref):
    both = jnp.sum(back_ref[...].astype(F32), axis=0)
    both += pltpu.roll(both, 6, 0)
    high = both.astype(BF16).astype(F32)
    sub = lax.broadcasted_iota(jnp.int32, both.shape, 0)
    piece = jnp.where(sub < 2, high, jnp.where(sub < 4, pltpu.roll(both - high, 2, 0), 0.0))
    out_ref[...] = jnp.broadcast_to(piece.astype(BF16)[None], out_ref.shape)


def append_kernel(got_ref, _, out_ref, held):
    groups = held.shape[0]
    both = got_ref[...].astype(F32)
    both += pltpu.roll(both, 6, 1)
    held[...] = jnp.sum(both.reshape(groups, -1, *both.shape[1:]), axis=1)
    rows = jnp.concatenate([held[:, 0], held[:, 1]], axis=1).astype(BF16)
    if out_ref.shape[1] > groups:
        rows = jnp.concatenate([rows, jnp.zeros((out_ref.shape[1] - groups, rows.shape[1]), BF16)], 0)
    out_ref[...] = jnp.broadcast_to(rows[None], out_ref.shape)


def finish_kernel(got_ref, w_ref, table_ref):
    rows = w_ref.shape[0]
    total = got_ref[0, :rows].astype(F32)
    for p in range(1, got_ref.shape[0]):
        total += got_ref[p, :rows].astype(F32)
    w_ref[...] = total
    for p in range(got_ref.shape[0]):
        table_ref[:, p] = got_ref[p, rows : rows + table_ref.shape[0]].astype(F32)


def whole(shape):
    return pl.BlockSpec(shape, lambda *_: (0,) * len(shape))


def params(mib):
    return pltpu.CompilerParams(vmem_limit_bytes=mib << 20)


def cost(flops, moved):
    return pl.CostEstimate(flops=flops, bytes_accessed=moved, transcendentals=0)


def local(tokens_in, w_in, filter_bank, lag_blocks, filter_ids, grad_out):
    chan, tok = grad_out.shape
    depth = tokens_in.shape[1]
    peers = lax.axis_size("ctx")
    blocks = tok * peers // BLK
    groups, stored, span = filter_bank.shape
    entries = lag_blocks.shape[1]
    share = depth // peers
    pairs = stored // 2 + 1
    group = (lax.axis_index("ch") // (lax.axis_size("ch") // groups)).astype(jnp.int32)[None]
    weights = jnp.transpose(w_in, (1, 2, 0)).reshape(3 * chan, depth)

    wide = 256
    proj, send = pl.pallas_call(
        project_kernel,
        grid=(tok // wide,),
        in_specs=[
            whole((3 * chan, depth)),
            pl.BlockSpec((wide, depth), lambda i: (i, 0)),
            pl.BlockSpec((chan, wide), lambda i: (0, i)),
        ],
        out_specs=[
            pl.BlockSpec((3 * chan, wide), lambda i: (0, i)),
            pl.BlockSpec((chan // 8, 2, 8, wide), lambda i: (0, 0, 0, i)),
        ],
        out_shape=[
            jax.ShapeDtypeStruct((3 * chan, tok), BF16),
            jax.ShapeDtypeStruct((chan // 8, 2, 8, tok), BF16),
        ],
        compiler_params=params(60),
        cost_estimate=cost(6 * chan * depth * tok, 2 * depth * (tok + 3 * chan)),
        name="project",
    )(weights, tokens_in, grad_out)
    rhs = pl.pallas_call(
        matrices_kernel,
        grid_spec=pltpu.PrefetchScalarGridSpec(
            num_scalar_prefetch=2,
            grid=(1,),
            in_specs=[pl.BlockSpec((1, stored, span), lambda i, g, ids: (g[0], 0, 0))],
            out_specs=whole((pairs, 2 * BLK, 2 * BLK)),
            scratch_shapes=[pltpu.VMEM((stored, span), F32)],
        ),
        out_shape=jax.ShapeDtypeStruct((pairs, 2 * BLK, 2 * BLK), BF16),
        compiler_params=params(60),
        cost_estimate=cost(pairs * 40 * BLK * BLK, pairs * 8 * BLK * BLK),
        name="matrices",
    )(group, filter_ids, filter_bank)
    seen = lax.all_to_all(send.reshape(peers, 8, tok), "ctx", 0, 0)
    back = pl.pallas_call(
        convolve_kernel,
        grid_spec=pltpu.PrefetchScalarGridSpec(
            num_scalar_prefetch=3,
            grid=(1,),
            in_specs=[whole((peers, 8, tok)), whole((pairs, 2 * BLK, 2 * BLK))],
            out_specs=whole((peers, 8, tok + BLK)),
            scratch_shapes=[
                pltpu.VMEM((blocks * 8, 2 * BLK), BF16),
                pltpu.VMEM((2 * pairs, 2 * blocks, 8, BLK), F32),
                pltpu.VMEM((blocks, 8, BLK), F32),
                pltpu.VMEM((2 * blocks, 8, BLK), F32),
                pltpu.VMEM((blocks, 8, BLK), F32),
                pltpu.VMEM((BLK, blocks * 8), BF16),
                pltpu.VMEM((stored, BLK, BLK), F32),
                pltpu.VMEM((stored, 8, span), F32),
            ],
        ),
        out_shape=jax.ShapeDtypeStruct((peers, 8, tok + BLK), BF16),
        compiler_params=params(60),
        cost_estimate=cost(pairs * 16 * blocks * 8 * BLK * BLK, peers * 32 * tok),
        name="convolve",
    )(group, lag_blocks, filter_ids, seen, rhs)
    got = lax.all_to_all(back, "ctx", 0, 0)
    lines = lax.axis_size("ch")
    piece = pl.pallas_call(
        spread_kernel,
        grid=(1,),
        in_specs=[pl.BlockSpec((peers, 8, BLK), lambda i: (0, 0, tok // BLK))],
        out_specs=whole((lines, 8, BLK)),
        out_shape=jax.ShapeDtypeStruct((lines, 8, BLK), BF16),
        compiler_params=params(60),
        name="spread",
    )(got)
    tables = lax.all_to_all(piece, "ch", 0, 0)
    chunk = 2
    rows = 3 * chan
    lines_in = -(-groups // 8) * 8
    gated, partial = pl.pallas_call(
        weights_kernel,
        grid=(peers // chunk,),
        in_specs=[
            whole((chan // 8, 2, 8, tok + BLK)),
            whole((rows, tok)),
            whole((chan, tok)),
            pl.BlockSpec((tok, chunk * share), lambda i: (0, i)),
        ],
        out_specs=[
            whole((chan, tok)),
            pl.BlockSpec((chunk, rows, share), lambda i: (i, 0, 0)),
        ],
        out_shape=[
            jax.ShapeDtypeStruct((chan, tok), BF16),
            jax.ShapeDtypeStruct((peers, rows + lines_in, share), BF16),
        ],
        scratch_shapes=[pltpu.VMEM((rows, tok), BF16)],
        compiler_params=params(60),
        cost_estimate=cost(6 * chan * depth * tok, 2 * depth * (tok + 6 * chan)),
        name="weights",
    )(got.reshape(chan // 8, 2, 8, tok + BLK), proj, grad_out, tokens_in)
    partial = pl.pallas_call(
        append_kernel,
        grid=(1,),
        in_specs=[whole((lines, 8, BLK)), pl.BlockSpec(memory_space=pl.ANY)],
        out_specs=pl.BlockSpec((peers, lines_in, share), lambda i: (0, rows // lines_in, 0)),
        out_shape=jax.ShapeDtypeStruct(partial.shape, BF16),
        scratch_shapes=[pltpu.VMEM((groups, 8, BLK), F32)],
        input_output_aliases={1: 0},
        compiler_params=params(60),
        name="append",
    )(tables, partial)
    parts = lax.all_to_all(partial, "ctx", 0, 0)
    w_grad, filter_grad = pl.pallas_call(
        finish_kernel,
        grid=(1,),
        in_specs=[whole(parts.shape)],
        out_specs=[whole((rows, share)), whole((groups, peers, share))],
        out_shape=[
            jax.ShapeDtypeStruct((rows, share), F32),
            jax.ShapeDtypeStruct((groups, peers, share), F32),
        ],
        compiler_params=params(60),
        name="finish",
    )(parts)
    w_grad = jnp.transpose(w_grad.reshape(3, chan, share), (2, 0, 1))
    return gated, w_grad, filter_grad


def solution(mesh):
    placed = (P("ctx", None), P(None, None, "ch"), P(), P(), P(), P("ch", "ctx"))
    return jax.shard_map(
        local,
        mesh=mesh,
        in_specs=placed,
        out_specs=(P("ch", "ctx"), P("ctx", None, "ch"), P()),
        check_vma=False,
    )
```

time: 983 us -> 142 us (0.14)
  waiting for transfers between devices: 691 us -> 10.5 us
  local copies, waits for them, and re-layouts: 245 us -> 1.32 us
  blocking collectives: 0 us -> 63.7 us
  Pallas kernels: 0 us -> 36.2 us
  starting transfers between devices: 0.34 us -> 28.7 us
  matrix products: 20.5 us -> 0 us
  between operations: 14 us -> 0.68 us
    psum x1 -> x0, waiting for transfers between devices: 465 us -> none  [local(): filter_grad = lax.psum(placed, ('ctx', 'ch'))]
    gather x192 -> x0, local copies, waits for them, and re-layouts: 180 us -> none
    all_gather x2 -> x0, waiting for transfers between devices: 120 us -> none  [the longest x1 64.8 us: local(): lax.all_gather(mixed, 'ctx', axis=1, tiled=True)]
    reduce_scatter x1 -> x0, waiting for transfers between devices: 106 us -> none  [local(): lax.psum_scatter(lax.dot_general(tokens_in, grad_proj, (((0,), (2,)), (()...]
    all_to_all x0 -> x2, blocking collectives: none -> 63.7 us  [the longest x1 48.3 us: local(): parts = lax.all_to_all(partial, 'ctx', 0, 0)]
    pallas_call x0 -> x7, Pallas kernels: none -> 36.2 us  [the longest x1 12.6 us: local(): pl.pallas_call(convolve_kernel, grid_spec=pltpu.PrefetchScalarGridSpec(nu...]
    all_to_all x0 -> x2, starting transfers between devices: none -> 28.7 us  [the longest x1 18.5 us: local(): tables = lax.all_to_all(piece, 'ch', 0, 0)]
    dot_general x7 -> x0, matrix products: 20.5 us -> none  [the longest x1 5.82 us: local(): lax.dot_general(tokens_in, grad_proj, (((0,), (2,)), ((), ())), preferred...]
  transfers between devices with their start and end apart: 4 -> 2, of which waited for: 4 -> 2; matrix products, arithmetic and copies ran while one was open for 2% -> 0% of each run, Pallas kernels for 0% -> 8%
where the time goes in v1:
time: 142 us; the launch traced here: 141 us
  blocking collectives  63.7 us (45%)
  Pallas kernels  36.2 us (25%)
  starting transfers between devices  28.7 us (20%)
  waiting for transfers between devices  10.5 us (7%)
    all_to_all x1, blocking collectives, local(): parts = lax.all_to_all(partial, 'ctx', 0, 0)  48.3 us
    all_to_all x1, starting transfers between devices, local(): tables = lax.all_to_all(piece, 'ch', 0, 0)  18.5 us
    all_to_all x1, blocking collectives, local(): got = lax.all_to_all(back, 'ctx', 0, 0)  15.4 us
    pallas_call x1, Pallas kernels, local(): pl.pallas_call(convolve_kernel, grid_spec=pltpu.PrefetchScalarGridSpec(nu...  12.6 us
    all_to_all x1, starting transfers between devices, local(): seen = lax.all_to_all(send.reshape(peers, 8, tok), 'ctx', 0, 0)  10.2 us
    pallas_call x1, Pallas kernels, local(): pl.pallas_call(weights_kernel, grid=(peers // chunk,), in_specs=[whole((c...  7.84 us
    pallas_call x1, Pallas kernels, local(): pl.pallas_call(project_kernel, grid=(tok // wide,), in_specs=[whole((3 *...  6.75 us
    all_to_all x1, waiting for transfers between devices, local(): seen = lax.all_to_all(send.reshape(peers, 8, tok), 'ctx', 0, 0)  6.29 us
  transfers between devices with their start and end apart: 2, of which 2 were waited for; matrix products, arithmetic and copies ran while one was open for 0% of the time, Pallas kernels for 8%

profile of v1, /device:TPU:1, one launch (start us, length us, event | category | flops | bytes accessed | tf_op | source)
XLA Modules:
  0.0 141.1 jit_solution(12625476134572662584)
XLA Ops:
  0.6 6.8 %project.1 = (bf16[192,768]{1,0:T(8,128)(2,1)}, bf16[8,2,8,768]{3,2,1,0:T(8,128)(2,1)}) custom-call(bf16[192,4096]{1,0:T(8,128)(2,1)} %bitcast.10, bf16[768,4096]{1,0:T(8,128)(2,1)} %tok_ref.3, bf16[64,768]{1,0:T(8,128)(2,1)} %cot_ref.3), custom_call_target="tpu_custom_call" | custom-call | flops 1207959552 | bytes 7864320 | tf_op jit(solution)/shard_map/project/pallas_call | solution.py:228
  7.4 10.2 %all-to-all-start = ((bf16[16,8,768]{2,1,0:T(8,128)(2,1)}), bf16[16,8,768]{2,1,0:T(8,128)(2,1)S(1)}, u32[]{:S(2)}, u32[]{:S(2)}) async-start(bf16[16,8,768]{2,1,0:T(8,128)(2,1)} %bitcast.11), calls=%async_computation | async-start | bytes 393216 | tf_op jit(solution)/shard_map/all_to_all | solution.py:262
  17.6 3.3 %matrices.1.rhs_ref = bf16[9,256,256]{2,1,0:T(8,128)(2,1)} custom-call(s32[1]{0:T(128)} %bitcast.group_ref, s32[24,32]{1,0:T(8,128)} %ids_ref.3, bf16[24,16,256]{2,1,0:T(8,128)(2,1)} %bank_ref.1), custom_call_target="tpu_custom_call" | custom-call | flops 5898240 | bytes 1179648 | tf_op jit(solution)/shard_map/matrices/pallas_call | solution.py:248
  20.9 6.3 %all-to-all-done.x_ref = bf16[16,8,768]{2,1,0:T(8,128)(2,1)S(1)} async-done(((bf16[16,8,768]{2,1,0:T(8,128)(2,1)}), bf16[16,8,768]{2,1,0:T(8,128)(2,1)S(1)}, u32[]{:S(2)}, u32[]{:S(2)}) %all-to-all-start) | async-done | bytes 196640 | tf_op jit(solution)/shard_map/all_to_all | solution.py:262
  27.2 0.0 copy-start.1
  27.2 0.7 copy-done.1
  27.9 12.6 %convolve.1 = bf16[16,8,896]{2,1,0:T(8,128)(2,1)} custom-call(s32[1]{0:T(128)} %bitcast.group_ref, s32[24,32]{1,0:T(8,128)} %lags_ref.1, s32[24,32]{1,0:T(8,128)} %ids_ref.3, bf16[16,8,768]{2,1,0:T(8,128)(2,1)} %copy-done.1, bf16[9,256,256]{2,1,0:T(8,128)(2,1)} %matrices.1.rhs_ref), custom_call_target="tpu_custom_call" | custom-call | flops 1811939328 | bytes 393216 | tf_op jit(solution)/shard_map/convolve/pallas_call | solution.py:263
  40.5 15.4 %all_to_all.20.back_ref = bf16[16,8,896]{2,1,0:T(8,128)(2,1)} all-to-all(bf16[16,8,896]{2,1,0:T(8,128)(2,1)} %convolve.1), channel_id=1, replica_groups=mesh['ctx'=16,'ch'=48] {'ctx'}, dimensions={0} | all-to-all | bytes 458752 | tf_op jit(solution)/shard_map/all_to_all | solution.py:286
  55.9 1.4 %spread.1 = bf16[48,8,128]{2,1,0:T(8,128)(2,1)} custom-call(bf16[16,8,896]{2,1,0:T(8,128)(2,1)} %all_to_all.20.back_ref), custom_call_target="tpu_custom_call" | custom-call | tf_op jit(solution)/shard_map/spread/pallas_call | solution.py:288
  57.4 18.5 %all-to-all-start.2 = ((bf16[48,8,128]{2,1,0:T(8,128)(2,1)}), bf16[48,8,128]{2,1,0:T(8,128)(2,1)S(1)}, u32[]{:S(2)}, u32[]{:S(2)}) async-start(bf16[48,8,128]{2,1,0:T(8,128)(2,1)} %spread.1), calls=%async_computation.2 | async-start | bytes 196608 | tf_op jit(solution)/shard_map/all_to_all | solution.py:297
  75.8 7.8 %weights.1 = (bf16[64,768]{1,0:T(8,128)(2,1)}, bf16[16,216,256]{2,1,0:T(8,128)(2,1)}) custom-call(bf16[8,2,8,896]{3,2,1,0:T(8,128)(2,1)} %bitcast.9, bf16[192,768]{1,0:T(8,128)(2,1)} %get-tuple-element.10.proj_ref, bf16[64,768]{1,0:T(8,128)(2,1)} %cot_ref.3, bf16[768,4096]{1,0:T(8,128)(2,1)} %tok_ref.3), custom_call_target="tpu_custom_call" | custom-call | flops 1207959552 | bytes 9437184 | tf_op jit(solution)/shard_map/weights/pallas_call | solution.py:301
  83.7 4.2 %all-to-all-done.2.got_ref = bf16[48,8,128]{2,1,0:T(8,128)(2,1)S(1)} async-done(((bf16[48,8,128]{2,1,0:T(8,128)(2,1)}), bf16[48,8,128]{2,1,0:T(8,128)(2,1)S(1)}, u32[]{:S(2)}, u32[]{:S(2)}) %all-to-all-start.2) | async-done | bytes 98336 | tf_op jit(solution)/shard_map/all_to_all | solution.py:297
  87.9 0.0 copy-start
  87.9 0.6 copy-done
  88.5 1.7 %append.1 = bf16[16,216,256]{2,1,0:T(8,128)(2,1)} custom-call(bf16[48,8,128]{2,1,0:T(8,128)(2,1)} %copy-done, bf16[16,216,256]{2,1,0:T(8,128)(2,1)} %get-tuple-element.12._), custom_call_target="tpu_custom_call", output_to_operand_aliasing={{}: (1, {})} | custom-call | tf_op jit(solution)/shard_map/append/pallas_call | solution.py:323
  90.2 48.3 %all_to_all.21.got_ref = bf16[16,216,256]{2,1,0:T(8,128)(2,1)} all-to-all(bf16[16,216,256]{2,1,0:T(8,128)(2,1)} %append.1), channel_id=1, replica_groups=mesh['ctx'=16,'ch'=48] {'ctx'}, dimensions={0} | all-to-all | bytes 3538944 | tf_op jit(solution)/shard_map/all_to_all | solution.py:334
  138.5 2.6 %finish.1 = (f32[192,256]{1,0:T(8,128)}, f32[24,16,256]{2,1,0:T(8,128)}) custom-call(bf16[16,216,256]{2,1,0:T(8,128)(2,1)} %all_to_all.21.got_ref), custom_call_target="tpu_custom_call" | custom-call | tf_op jit(solution)/shard_map/finish/pallas_call | solution.py:335
Async XLA Ops:
  7.4 19.8 %all-to-all-start = ((bf16[16,8,768]{2,1,0:T(8,128)(2,1)}), bf16[16,8,768]{2,1,0:T(8,128)(2,1)S(1)}, u32[]{:S(2)}, u32[]{:S(2)}) async-start(bf16[16,8,768]{2,1,0:T(8,128)(2,1)} %bitcast.11), calls=%async_computation | async-start | bytes 393216 | tf_op jit(solution)/shard_map/all_to_all | solution.py:262
  27.2 0.7 copy-start.1
  57.4 30.5 %all-to-all-start.2 = ((bf16[48,8,128]{2,1,0:T(8,128)(2,1)}), bf16[48,8,128]{2,1,0:T(8,128)(2,1)S(1)}, u32[]{:S(2)}, u32[]{:S(2)}) async-start(bf16[48,8,128]{2,1,0:T(8,128)(2,1)} %spread.1), calls=%async_computation.2 | async-start | bytes 196608 | tf_op jit(solution)/shard_map/all_to_all | solution.py:297
  87.9 0.6 copy-start

commit v2 on v1

--- a/solution.py
+++ b/solution.py
@@ -6,6 +6,7 @@
 from jax.sharding import PartitionSpec as P
 
 BLK = 128
+CHUNK = 24
 HALF = 4
 BF16, F32 = jnp.bfloat16, jnp.float32
 
@@ -14,21 +15,33 @@
     return lax.broadcasted_iota(jnp.int32, shape, len(shape) - 2) < HALF
 
 
-def project_kernel(w_ref, tok_ref, cot_ref, proj_ref, send_ref):
-    chan = cot_ref.shape[0]
-    width = tok_ref.shape[0]
-    proj = lax.dot_general(
+def project_kernel(w_ref, tok_ref, cot_ref, proj_ref, send_ref, acc):
+    chan, tok = cot_ref.shape
+    step = pl.program_id(0)
+    part = lax.dot_general(
         w_ref[...], tok_ref[...], (((1,), (1,)), ((), ())), preferred_element_type=F32
-    ).astype(BF16)
-    proj_ref[...] = proj
-    wide = proj.astype(F32)
-    mixed = wide[chan : 2 * chan] * wide[2 * chan :]
-    grad_conv = cot_ref[...].astype(F32) * wide[:chan]
-    mixed = mixed.reshape(chan // 8, 8, width)
-    grad_conv = grad_conv.reshape(chan // 8, 8, width)
-    low = low_rows(mixed.shape)
-    send_ref[:, 0] = jnp.where(low, mixed, pltpu.roll(grad_conv, HALF, 1)).astype(BF16)
-    send_ref[:, 1] = jnp.where(low, pltpu.roll(mixed, HALF, 1), grad_conv).astype(BF16)
+    )
+
+    @pl.when(step == 0)
+    def _():
+        acc[...] = part
+
+    @pl.when(step > 0)
+    def _():
+        acc[...] += part
+
+    @pl.when(step == pl.num_programs(0) - 1)
+    def _():
+        proj = acc[...].astype(BF16)
+        proj_ref[...] = proj
+        wide = proj.astype(F32)
+        mixed = wide[chan : 2 * chan] * wide[2 * chan :]
+        grad_conv = cot_ref[...].astype(F32) * wide[:chan]
+        mixed = mixed.reshape(chan // 8, 8, tok)
+        grad_conv = grad_conv.reshape(chan // 8, 8, tok)
+        low = low_rows(mixed.shape)
+        send_ref[:, 0] = jnp.where(low, mixed, pltpu.roll(grad_conv, HALF, 1)).astype(BF16)
+        send_ref[:, 1] = jnp.where(low, pltpu.roll(mixed, HALF, 1), grad_conv).astype(BF16)
 
 
 def matrices_kernel(group_ref, ids_ref, bank_ref, rhs_ref, bank_f32):
@@ -80,19 +93,19 @@
         both = jnp.dot(lhs[...], rhs_ref[pair], preferred_element_type=F32)
         for j in (0, 1):
             half = both[:, j * BLK : (j + 1) * BLK].reshape(blocks, 8, BLK)
-            prod[2 * pair + j, blocks:] = half
-            prod[2 * pair + j, :blocks] = jnp.zeros((blocks, 8, BLK), F32)
+            prod[2 * pair + j, CHUNK:] = half
+            prod[2 * pair + j, :CHUNK] = jnp.zeros((CHUNK, 8, BLK), F32)
         return carry
 
-    lax.fori_loop(0, pairs, product, 0)
-    chunk = 24
-    for start in range(0, blocks, chunk):
+    lax.fori_loop(0, pairs, product, 0, unroll=True)
+    for start in range(0, blocks, CHUNK):
 
         def add(k, acc):
-            return acc + prod[ids_ref[group, k], pl.ds(blocks + start - lags_ref[group, k], chunk)]
-
-        acc = prod[stored, blocks + start : blocks + start + chunk]
-        res[start : start + chunk] = lax.fori_loop(1, entries, add, acc)
+            first = jnp.maximum(CHUNK + start - lags_ref[group, k], 0)
+            return acc + prod[ids_ref[group, k], pl.ds(first, CHUNK)]
+
+        acc = prod[stored, CHUNK + start : 2 * CHUNK + start]
+        res[start : start + CHUNK] = lax.fori_loop(1, entries, add, acc, unroll=True)
     for i in range(blocks):
         both = jnp.where(low, res[i], res[blocks - 1 - i])
         out_ref[i // per, :, (i % per) * BLK : (i % per + 1) * BLK] = both.astype(BF16)
@@ -109,27 +122,33 @@
     padded[:blocks] = jnp.zeros((blocks, 8, BLK), F32)
     for i in range(blocks):
         tile = x_ref[i // per, :, (i % per) * BLK : (i % per + 1) * BLK].astype(F32)
-        padded[blocks + i] = jnp.where(low, tile, 0.0)
-        cots[i] = jnp.where(low, pltpu.roll(tile, HALF, 0), 0.0)
+        other = pltpu.roll(tile, HALF, 0)
+        padded[blocks + i] = jnp.where(low, tile, other)
+        cots[0, i] = jnp.where(low, other, 0.0)
+        cots[1, i] = jnp.where(low, 0.0, tile)
     step = BLK // 8
-    for j in range(blocks // step):
-        rows = cots[j * step : (j + 1) * step].reshape(BLK, BLK)
-        turned[:, j * BLK : (j + 1) * BLK] = rows.T.astype(BF16)
+    for h in (0, 1):
+        for j in range(blocks // step):
+            rows = cots[h, j * step : (j + 1) * step].reshape(BLK, BLK)
+            turned[h * BLK : (h + 1) * BLK, j * BLK : (j + 1) * BLK] = rows.T.astype(BF16)
     sums[...] = jnp.zeros(sums.shape, F32)
     row = lax.broadcasted_iota(jnp.int32, (BLK, BLK), 0)
     col = lax.broadcasted_iota(jnp.int32, (BLK, BLK), 1)
-
-    def pair(p, carry):
-        k = 2 * p
-        shifted = [padded[pl.ds(blocks - lags_ref[group, k + j], blocks)] for j in (0, 1)]
-        shifted = [s.reshape(blocks * 8, BLK).astype(BF16) for s in shifted]
-        both = jnp.dot(turned[...], jnp.concatenate(shifted, 1), preferred_element_type=F32)
-        keep = (row >= col) | (k > 0)
-        sums[ids_ref[group, k]] += jnp.where(keep, both[:, :BLK], 0.0)
-        sums[ids_ref[group, k + 1]] += both[:, BLK:]
+    low_all = low_rows((blocks, 8, BLK))
+
+    def four(p, carry):
+        sides = []
+        for j in (0, 2):
+            top, bottom = (padded[pl.ds(blocks - lags_ref[group, 4 * p + j + h], blocks)] for h in (0, 1))
+            sides.append(jnp.where(low_all, top, bottom).reshape(blocks * 8, BLK).astype(BF16))
+        both = jnp.dot(turned[...], jnp.concatenate(sides, 1), preferred_element_type=F32)
+        keep = (row >= col) | (p > 0)
+        for j in range(4):
+            part = both[(j % 2) * BLK : (j % 2 + 1) * BLK, (j // 2) * BLK : (j // 2 + 1) * BLK]
+            sums[ids_ref[group, 4 * p + j]] += jnp.where(keep, part, 0.0) if j == 0 else part
         return carry
 
-    lax.fori_loop(0, entries // 2, pair, 0)
+    lax.fori_loop(0, entries // 4, four, 0, unroll=True)
     for f in range(stored):
         mat = jnp.concatenate([jnp.zeros((BLK, BLK), F32), sums[f].T], 1)
         total = mat[:8]
@@ -223,25 +242,26 @@
     pairs = stored // 2 + 1
     group = (lax.axis_index("ch") // (lax.axis_size("ch") // groups)).astype(jnp.int32)[None]
     weights = jnp.transpose(w_in, (1, 2, 0)).reshape(3 * chan, depth)
-
-    wide = 256
+    weights = pltpu.with_memory_space_constraint(weights, pltpu.HBM)
+    tokens_in = pltpu.with_memory_space_constraint(tokens_in, pltpu.HBM)
+    grad_out = pltpu.with_memory_space_constraint(grad_out, pltpu.HBM)
+
+    deep = depth // 4
     proj, send = pl.pallas_call(
         project_kernel,
-        grid=(tok // wide,),
+        grid=(depth // deep,),
         in_specs=[
-            whole((3 * chan, depth)),
-            pl.BlockSpec((wide, depth), lambda i: (i, 0)),
-            pl.BlockSpec((chan, wide), lambda i: (0, i)),
-        ],
-        out_specs=[
-            pl.BlockSpec((3 * chan, wide), lambda i: (0, i)),
-            pl.BlockSpec((chan // 8, 2, 8, wide), lambda i: (0, 0, 0, i)),
-        ],
+            pl.BlockSpec((3 * chan, deep), lambda i: (0, i)),
+            pl.BlockSpec((tok, deep), lambda i: (0, i)),
+            whole((chan, tok)),
+        ],
+        out_specs=[whole((3 * chan, tok)), whole((chan // 8, 2, 8, tok))],
+        scratch_shapes=[pltpu.VMEM((3 * chan, tok), F32)],
         out_shape=[
             jax.ShapeDtypeStruct((3 * chan, tok), BF16),
             jax.ShapeDtypeStruct((chan // 8, 2, 8, tok), BF16),
         ],
-        compiler_params=params(60),
+        compiler_params=params(20),
         cost_estimate=cost(6 * chan * depth * tok, 2 * depth * (tok + 3 * chan)),
         name="project",
     )(weights, tokens_in, grad_out)
@@ -255,7 +275,7 @@
             scratch_shapes=[pltpu.VMEM((stored, span), F32)],
         ),
         out_shape=jax.ShapeDtypeStruct((pairs, 2 * BLK, 2 * BLK), BF16),
-        compiler_params=params(60),
+        compiler_params=params(8),
         cost_estimate=cost(pairs * 40 * BLK * BLK, pairs * 8 * BLK * BLK),
         name="matrices",
     )(group, filter_ids, filter_bank)
@@ -269,17 +289,17 @@
             out_specs=whole((peers, 8, tok + BLK)),
             scratch_shapes=[
                 pltpu.VMEM((blocks * 8, 2 * BLK), BF16),
-                pltpu.VMEM((2 * pairs, 2 * blocks, 8, BLK), F32),
+                pltpu.VMEM((2 * pairs, blocks + CHUNK, 8, BLK), F32),
                 pltpu.VMEM((blocks, 8, BLK), F32),
                 pltpu.VMEM((2 * blocks, 8, BLK), F32),
-                pltpu.VMEM((blocks, 8, BLK), F32),
-                pltpu.VMEM((BLK, blocks * 8), BF16),
+                pltpu.VMEM((2, blocks, 8, BLK), F32),
+                pltpu.VMEM((2 * BLK, blocks * 8), BF16),
                 pltpu.VMEM((stored, BLK, BLK), F32),
                 pltpu.VMEM((stored, 8, span), F32),
             ],
         ),
         out_shape=jax.ShapeDtypeStruct((peers, 8, tok + BLK), BF16),
-        compiler_params=params(60),
+        compiler_params=params(24),
         cost_estimate=cost(pairs * 16 * blocks * 8 * BLK * BLK, peers * 32 * tok),
         name="convolve",
     )(group, lag_blocks, filter_ids, seen, rhs)
@@ -291,7 +311,7 @@
         in_specs=[pl.BlockSpec((peers, 8, BLK), lambda i: (0, 0, tok // BLK))],
         out_specs=whole((lines, 8, BLK)),
         out_shape=jax.ShapeDtypeStruct((lines, 8, BLK), BF16),
-        compiler_params=params(60),
+        compiler_params=params(4),
         name="spread",
     )(got)
     tables = lax.all_to_all(piece, "ch", 0, 0)
@@ -316,7 +336,7 @@
             jax.ShapeDtypeStruct((peers, rows + lines_in, share), BF16),
         ],
         scratch_shapes=[pltpu.VMEM((rows, tok), BF16)],
-        compiler_params=params(60),
+        compiler_params=params(20),
         cost_estimate=cost(6 * chan * depth * tok, 2 * depth * (tok + 6 * chan)),
         name="weights",
     )(got.reshape(chan // 8, 2, 8, tok + BLK), proj, grad_out, tokens_in)
@@ -328,7 +348,7 @@
         out_shape=jax.ShapeDtypeStruct(partial.shape, BF16),
         scratch_shapes=[pltpu.VMEM((groups, 8, BLK), F32)],
         input_output_aliases={1: 0},
-        compiler_params=params(60),
+        compiler_params=params(8),
         name="append",
     )(tables, partial)
     parts = lax.all_to_all(partial, "ctx", 0, 0)
@@ -341,7 +361,7 @@
             jax.ShapeDtypeStruct((rows, share), F32),
             jax.ShapeDtypeStruct((groups, peers, share), F32),
         ],
-        compiler_params=params(60),
+        compiler_params=params(10),
         name="finish",
     )(parts)
     w_grad = jnp.transpose(w_grad.reshape(3, chan, share), (2, 0, 1))

time: 142 us -> 127 us (0.89)
  Pallas kernels: 36.2 us -> 21.5 us
  waiting for transfers between devices: 10.5 us -> 13.2 us
  blocking collectives: 63.7 us -> 62 us
    pallas_call x1, Pallas kernels: 12.6 us -> 4.99 us  [local(): pl.pallas_call(convolve_kernel, grid_spec=pltpu.PrefetchScalarGridSpec(nu...]
    pallas_call x1, Pallas kernels: 3.32 us -> 1.46 us  [local(): pl.pallas_call(matrices_kernel, grid_spec=pltpu.PrefetchScalarGridSpec(nu...]
    all_to_all x1, waiting for transfers between devices: 6.29 us -> 8.12 us  [local(): seen = lax.all_to_all(send.reshape(peers, 8, tok), 'ctx', 0, 0)]
    pallas_call x1, Pallas kernels: 1.65 us -> 0.06 us  [local(): pl.pallas_call(append_kernel, grid=(1,), in_specs=[whole((lines, 8, BLK))...]
    pallas_call x1, Pallas kernels: 2.6 us -> 1.13 us  [local(): pl.pallas_call(finish_kernel, grid=(1,), in_specs=[whole(parts.shape)], o...]
  transfers between devices with their start and end apart: 2 -> 2, of which waited for: 2 -> 2; matrix products, arithmetic and copies ran while one was open for 0% -> 0% of each run, Pallas kernels for 8% -> 7%
where the time goes in v2:
time: 127 us; the launch traced here: 126 us
  blocking collectives  62 us (49%)
  starting transfers between devices  28.8 us (23%)
  Pallas kernels  21.5 us (17%)
  waiting for transfers between devices  13.2 us (10%)
    all_to_all x1, blocking collectives, local(): parts = lax.all_to_all(partial, 'ctx', 0, 0)  46.9 us
    all_to_all x1, starting transfers between devices, local(): tables = lax.all_to_all(piece, 'ch', 0, 0)  18.4 us
    all_to_all x1, blocking collectives, local(): got = lax.all_to_all(back, 'ctx', 0, 0)  15.1 us
    all_to_all x1, starting transfers between devices, local(): seen = lax.all_to_all(send.reshape(peers, 8, tok), 'ctx', 0, 0)  10.3 us
    all_to_all x1, waiting for transfers between devices, local(): seen = lax.all_to_all(send.reshape(peers, 8, tok), 'ctx', 0, 0)  8.12 us
    pallas_call x1, Pallas kernels, local(): pl.pallas_call(weights_kernel, grid=(peers // chunk,), in_specs=[whole((c...  6.99 us
    pallas_call x1, Pallas kernels, local(): pl.pallas_call(project_kernel, grid=(depth // deep,), in_specs=[pl.BlockS...  6.21 us
    all_to_all x1, waiting for transfers between devices, local(): tables = lax.all_to_all(piece, 'ch', 0, 0)  5.06 us
  transfers between devices with their start and end apart: 2, of which 2 were waited for; matrix products, arithmetic and copies ran while one was open for 0% of the time, Pallas kernels for 7%

profile of v2, /device:TPU:1, one launch (start us, length us, event | category | flops | bytes accessed | tf_op | source)
XLA Modules:
  0.0 126.2 jit_solution(12175168998768605840)
XLA Ops:
  0.6 0.0 copy-start
  0.6 0.0 copy-start.1
  0.7 6.2 %project.1 = (bf16[192,768]{1,0:T(8,128)(2,1)S(1)}, bf16[8,2,8,768]{3,2,1,0:T(8,128)(2,1)}) custom-call(bf16[192,4096]{1,0:T(8,128)(2,1)} %bitcast.10, bf16[768,4096]{1,0:T(8,128)(2,1)} %tok_ref.3, bf16[64,768]{1,0:T(8,128)(2,1)} %cot_ref.3), custom_call_target="tpu_custom_call" | custom-call | flops 1207959552 | bytes 7864320 | tf_op jit(solution)/shard_map/project/pallas_call | solution.py:250
  6.9 0.0 copy-start.2
  6.9 10.3 %all-to-all-start = ((bf16[16,8,768]{2,1,0:T(8,128)(2,1)}), bf16[16,8,768]{2,1,0:T(8,128)(2,1)S(1)}, u32[]{:S(2)}, u32[]{:S(2)}) async-start(bf16[16,8,768]{2,1,0:T(8,128)(2,1)} %bitcast.3), calls=%async_computation | async-start | bytes 393216 | tf_op jit(solution)/shard_map/all_to_all | solution.py:282
  17.2 0.0 copy-done
  17.2 0.0 copy-done.1
  17.3 1.5 %matrices.1.rhs_ref = bf16[9,256,256]{2,1,0:T(8,128)(2,1)S(1)} custom-call(s32[1]{0:T(128)} %bitcast.group_ref, s32[24,32]{1,0:T(8,128)S(1)} %copy-done.1, bf16[24,16,256]{2,1,0:T(8,128)(2,1)S(1)} %copy-done), custom_call_target="tpu_custom_call" | custom-call | flops 5898240 | bytes 1179648 | tf_op jit(solution)/shard_map/matrices/pallas_call | solution.py:268
  18.7 8.1 %all-to-all-done.x_ref = bf16[16,8,768]{2,1,0:T(8,128)(2,1)S(1)} async-done(((bf16[16,8,768]{2,1,0:T(8,128)(2,1)}), bf16[16,8,768]{2,1,0:T(8,128)(2,1)S(1)}, u32[]{:S(2)}, u32[]{:S(2)}) %all-to-all-start) | async-done | bytes 196640 | tf_op jit(solution)/shard_map/all_to_all | solution.py:282
  26.8 0.0 copy-done.2
  26.8 5.0 %convolve.1 = bf16[16,8,896]{2,1,0:T(8,128)(2,1)S(1)} custom-call(s32[1]{0:T(128)} %bitcast.group_ref, s32[24,32]{1,0:T(8,128)S(1)} %copy-done.2, s32[24,32]{1,0:T(8,128)S(1)} %copy-done.1, bf16[16,8,768]{2,1,0:T(8,128)(2,1)S(1)} %all-to-all-done.x_ref, bf16[9,256,256]{2,1,0:T(8,128)(2,1)S(1)} %matrices.1.rhs_ref), custom_call_target="tpu_custom_call" | custom-call | flops 1811939328 | bytes 393216 | tf_op jit(solution)/shard_map/convolve/pallas_call | solution.py:283
  31.8 15.1 %all_to_all.20.back_ref = bf16[16,8,896]{2,1,0:T(8,128)(2,1)S(1)} all-to-all(bf16[16,8,896]{2,1,0:T(8,128)(2,1)S(1)} %convolve.1), channel_id=1, replica_groups=mesh['ctx'=16,'ch'=48] {'ctx'}, dimensions={0} | all-to-all | bytes 458752 | tf_op jit(solution)/shard_map/all_to_all | solution.py:306
  47.0 0.7 spread.1
  47.6 18.4 %all-to-all-start.2 = ((bf16[48,8,128]{2,1,0:T(8,128)(2,1)}), bf16[48,8,128]{2,1,0:T(8,128)(2,1)S(1)}, u32[]{:S(2)}, u32[]{:S(2)}) async-start(bf16[48,8,128]{2,1,0:T(8,128)(2,1)} %spread.1), calls=%async_computation.2 | async-start | bytes 196608 | tf_op jit(solution)/shard_map/all_to_all | solution.py:317
  66.1 7.0 %weights.1 = (bf16[64,768]{1,0:T(8,128)(2,1)}, bf16[16,216,256]{2,1,0:T(8,128)(2,1)S(1)}) custom-call(bf16[8,2,8,896]{3,2,1,0:T(8,128)(2,1)S(1)} %bitcast.9, bf16[192,768]{1,0:T(8,128)(2,1)S(1)} %get-tuple-element.10.proj_ref, bf16[64,768]{1,0:T(8,128)(2,1)} %cot_ref.3, bf16[768,4096]{1,0:T(8,128)(2,1)} %tok_ref.3), custom_call_target="tpu_custom_call" | custom-call | flops 1207959552 | bytes 9437184 | tf_op jit(solution)/shard_map/weights/pallas_call | solution.py:321
  73.1 5.1 %all-to-all-done.2.got_ref = bf16[48,8,128]{2,1,0:T(8,128)(2,1)S(1)} async-done(((bf16[48,8,128]{2,1,0:T(8,128)(2,1)}), bf16[48,8,128]{2,1,0:T(8,128)(2,1)S(1)}, u32[]{:S(2)}, u32[]{:S(2)}) %all-to-all-start.2) | async-done | bytes 98336 | tf_op jit(solution)/shard_map/all_to_all | solution.py:317
  78.1 0.1 append.1
  78.2 46.9 %all_to_all.21.got_ref = bf16[16,216,256]{2,1,0:T(8,128)(2,1)S(1)} all-to-all(bf16[16,216,256]{2,1,0:T(8,128)(2,1)S(1)} %append.1), channel_id=1, replica_groups=mesh['ctx'=16,'ch'=48] {'ctx'}, dimensions={0} | all-to-all | bytes 3538944 | tf_op jit(solution)/shard_map/all_to_all | solution.py:354
  125.1 1.1 finish.1
Async XLA Ops:
  0.6 16.6 %copy-start = (bf16[24,16,256]{2,1,0:T(8,128)(2,1)S(1)}, bf16[24,16,256]{2,1,0:T(8,128)(2,1)}, u32[]{:S(2)}) copy-start(bf16[24,16,256]{2,1,0:T(8,128)(2,1)} %bank_ref.1) | copy-start | bytes 589828
  0.6 16.6 %copy-start.1 = (s32[24,32]{1,0:T(8,128)S(1)}, s32[24,32]{1,0:T(8,128)}, u32[]{:S(2)}) copy-start(s32[24,32]{1,0:T(8,128)} %ids_ref.3) | copy-start | bytes 9220
  6.9 20.0 %copy-start.2 = (s32[24,32]{1,0:T(8,128)S(1)}, s32[24,32]{1,0:T(8,128)}, u32[]{:S(2)}) copy-start(s32[24,32]{1,0:T(8,128)} %lags_ref.1) | copy-start | bytes 9220
  6.9 20.0 %all-to-all-start = ((bf16[16,8,768]{2,1,0:T(8,128)(2,1)}), bf16[16,8,768]{2,1,0:T(8,128)(2,1)S(1)}, u32[]{:S(2)}, u32[]{:S(2)}) async-start(bf16[16,8,768]{2,1,0:T(8,128)(2,1)} %bitcast.3), calls=%async_computation | async-start | bytes 393216 | tf_op jit(solution)/shard_map/all_to_all | solution.py:282
  47.6 30.5 %all-to-all-start.2 = ((bf16[48,8,128]{2,1,0:T(8,128)(2,1)}), bf16[48,8,128]{2,1,0:T(8,128)(2,1)S(1)}, u32[]{:S(2)}, u32[]{:S(2)}) async-start(bf16[48,8,128]{2,1,0:T(8,128)(2,1)} %spread.1), calls=%async_computation.2 | async-start | bytes 196608 | tf_op jit(solution)/shard_map/all_to_all | solution.py:317

commit v3 on v2

--- a/solution.py
+++ b/solution.py
@@ -7,6 +7,7 @@
 
 BLK = 128
 CHUNK = 24
+LINE = 4
 HALF = 4
 BF16, F32 = jnp.bfloat16, jnp.float32
 
@@ -158,14 +159,15 @@
     total = folded[:, 0]
     for s in range(1, 8):
         total += pltpu.roll(folded[:, s], 2 * BLK - s, 1)
-    high = total.astype(BF16).astype(F32)
-    rest = total - high
     sub = lax.broadcasted_iota(jnp.int32, (8, BLK), 0)
-    for p in range(peers):
+    per_line = stored // LINE
+    for x in range(LINE):
         piece = jnp.zeros((8, BLK), F32)
-        for r, part in enumerate((high[:, :BLK], high[:, BLK:], rest[:, :BLK], rest[:, BLK:])):
-            piece = jnp.where(sub == r, part[p : p + 1], piece)
-        out_ref[p, :, tok:] = piece.astype(BF16)
+        for r in range(2 * per_line):
+            f = (r // 2) * LINE + x
+            piece = jnp.where(sub == r, total[f : f + 1, (r % 2) * BLK : (r % 2 + 1) * BLK], piece)
+        for p in range(x, peers, LINE):
+            out_ref[p, :, tok:] = piece.astype(BF16)
 
 
 def weights_kernel(back_ref, proj_ref, cot_ref, tok_ref, gated_ref, out_ref, grads):
@@ -191,32 +193,33 @@
 
 def spread_kernel(back_ref, out_ref):
     both = jnp.sum(back_ref[...].astype(F32), axis=0)
-    both += pltpu.roll(both, 6, 0)
-    high = both.astype(BF16).astype(F32)
-    sub = lax.broadcasted_iota(jnp.int32, both.shape, 0)
-    piece = jnp.where(sub < 2, high, jnp.where(sub < 4, pltpu.roll(both - high, 2, 0), 0.0))
-    out_ref[...] = jnp.broadcast_to(piece.astype(BF16)[None], out_ref.shape)
+    out_ref[...] = jnp.broadcast_to(both.astype(BF16)[None], out_ref.shape)
 
 
 def append_kernel(got_ref, _, out_ref, held):
     groups = held.shape[0]
     both = got_ref[...].astype(F32)
-    both += pltpu.roll(both, 6, 1)
     held[...] = jnp.sum(both.reshape(groups, -1, *both.shape[1:]), axis=1)
-    rows = jnp.concatenate([held[:, 0], held[:, 1]], axis=1).astype(BF16)
-    if out_ref.shape[1] > groups:
-        rows = jnp.concatenate([rows, jnp.zeros((out_ref.shape[1] - groups, rows.shape[1]), BF16)], 0)
-    out_ref[...] = jnp.broadcast_to(rows[None], out_ref.shape)
-
-
-def finish_kernel(got_ref, w_ref, table_ref):
-    rows = w_ref.shape[0]
-    total = got_ref[0, :rows].astype(F32)
-    for p in range(1, got_ref.shape[0]):
-        total += got_ref[p, :rows].astype(F32)
-    w_ref[...] = total
-    for p in range(got_ref.shape[0]):
-        table_ref[:, p] = got_ref[p, rows : rows + table_ref.shape[0]].astype(F32)
+    lines_in = out_ref.shape[1] // (held.shape[1] // 2)
+    for j in range(held.shape[1] // 2):
+        rows = jnp.concatenate([held[:, 2 * j], held[:, 2 * j + 1]], axis=1).astype(BF16)
+        rows = jnp.broadcast_to(rows[None], (out_ref.shape[0], *rows.shape))
+        out_ref[:, j * lines_in : j * lines_in + groups] = rows
+
+
+def fold_kernel(got_ref, w_ref, table_ref):
+    lines, rows = w_ref.shape[:2]
+    for y in range(lines):
+        total = got_ref[0, y * rows : (y + 1) * rows].astype(F32)
+        for x in range(1, got_ref.shape[0]):
+            total += got_ref[x, y * rows : (y + 1) * rows].astype(F32)
+        w_ref[y] = total.astype(BF16)
+    groups, stored = table_ref.shape[:2]
+    per_line = stored // LINE
+    lines_in = (got_ref.shape[1] - lines * rows) // per_line
+    for f in range(stored):
+        start = lines * rows + (f // LINE) * lines_in
+        table_ref[:, f] = got_ref[f % LINE, start : start + groups].astype(F32)
 
 
 def whole(shape):
@@ -304,20 +307,22 @@
         name="convolve",
     )(group, lag_blocks, filter_ids, seen, rhs)
     got = lax.all_to_all(back, "ctx", 0, 0)
-    lines = lax.axis_size("ch")
+    wide = lax.axis_size("ch")
     piece = pl.pallas_call(
         spread_kernel,
         grid=(1,),
         in_specs=[pl.BlockSpec((peers, 8, BLK), lambda i: (0, 0, tok // BLK))],
-        out_specs=whole((lines, 8, BLK)),
-        out_shape=jax.ShapeDtypeStruct((lines, 8, BLK), BF16),
+        out_specs=whole((wide, 8, BLK)),
+        out_shape=jax.ShapeDtypeStruct((wide, 8, BLK), BF16),
         compiler_params=params(4),
         name="spread",
     )(got)
     tables = lax.all_to_all(piece, "ch", 0, 0)
     chunk = 2
     rows = 3 * chan
-    lines_in = -(-groups // 8) * 8
+    lines = peers // LINE
+    half = LINE // chunk
+    extra = -(-groups // 8) * 8 * (stored // LINE)
     gated, partial = pl.pallas_call(
         weights_kernel,
         grid=(peers // chunk,),
@@ -329,11 +334,11 @@
         ],
         out_specs=[
             whole((chan, tok)),
-            pl.BlockSpec((chunk, rows, share), lambda i: (i, 0, 0)),
+            pl.BlockSpec((chunk, rows, share), lambda i: (i % half, i // half, 0)),
         ],
         out_shape=[
             jax.ShapeDtypeStruct((chan, tok), BF16),
-            jax.ShapeDtypeStruct((peers, rows + lines_in, share), BF16),
+            jax.ShapeDtypeStruct((LINE, lines * rows + extra, share), BF16),
         ],
         scratch_shapes=[pltpu.VMEM((rows, tok), BF16)],
         compiler_params=params(20),
@@ -343,27 +348,31 @@
     partial = pl.pallas_call(
         append_kernel,
         grid=(1,),
-        in_specs=[whole((lines, 8, BLK)), pl.BlockSpec(memory_space=pl.ANY)],
-        out_specs=pl.BlockSpec((peers, lines_in, share), lambda i: (0, rows // lines_in, 0)),
+        in_specs=[whole((wide, 8, BLK)), pl.BlockSpec(memory_space=pl.ANY)],
+        out_specs=pl.BlockSpec((LINE, extra, share), lambda i: (0, lines * rows // extra, 0)),
         out_shape=jax.ShapeDtypeStruct(partial.shape, BF16),
         scratch_shapes=[pltpu.VMEM((groups, 8, BLK), F32)],
         input_output_aliases={1: 0},
         compiler_params=params(8),
         name="append",
     )(tables, partial)
-    parts = lax.all_to_all(partial, "ctx", 0, 0)
-    w_grad, filter_grad = pl.pallas_call(
-        finish_kernel,
+    along_x = [[y * LINE + x for x in range(LINE)] for y in range(lines)]
+    along_y = [[y * LINE + x for y in range(lines)] for x in range(LINE)]
+    parts = lax.all_to_all(partial, "ctx", 0, 0, axis_index_groups=along_x)
+    folded, filter_grad = pl.pallas_call(
+        fold_kernel,
         grid=(1,),
         in_specs=[whole(parts.shape)],
-        out_specs=[whole((rows, share)), whole((groups, peers, share))],
+        out_specs=[whole((lines, rows, share)), whole((groups, stored, share))],
         out_shape=[
-            jax.ShapeDtypeStruct((rows, share), F32),
-            jax.ShapeDtypeStruct((groups, peers, share), F32),
-        ],
-        compiler_params=params(10),
-        name="finish",
+            jax.ShapeDtypeStruct((lines, rows, share), BF16),
+            jax.ShapeDtypeStruct((groups, stored, share), F32),
+        ],
+        compiler_params=params(12),
+        name="fold",
     )(parts)
+    sums = lax.all_to_all(folded, "ctx", 0, 0, axis_index_groups=along_y)
+    w_grad = jnp.sum(sums.astype(F32), axis=0)
     w_grad = jnp.transpose(w_grad.reshape(3, chan, share), (2, 0, 1))
     return gated, w_grad, filter_grad
 

time: 127 us -> 120 us (0.945)
  blocking collectives: 62 us -> 53.8 us
    all_to_all x1 -> x2, blocking collectives: 46.9 us -> 38.7 us  [the longest x1 24.7 us: local(): parts = lax.all_to_all(partial, 'ctx', 0, 0, axis_index_groups=along_x)]
where the time goes in v3:
time: 120 us; the launch traced here: 119 us
  blocking collectives  53.8 us (45%)
  starting transfers between devices  28.9 us (24%)
  Pallas kernels  21.5 us (18%)
  waiting for transfers between devices  13 us (11%)
    all_to_all x1, blocking collectives, local(): parts = lax.all_to_all(partial, 'ctx', 0, 0, axis_index_groups=along_x)  24.7 us
    all_to_all x1, starting transfers between devices, local(): tables = lax.all_to_all(piece, 'ch', 0, 0)  18.5 us
    all_to_all x1, blocking collectives, local(): got = lax.all_to_all(back, 'ctx', 0, 0)  15.1 us
    all_to_all x1, blocking collectives, local(): sums = lax.all_to_all(folded, 'ctx', 0, 0, axis_index_groups=along_y)  14 us
    all_to_all x1, starting transfers between devices, local(): seen = lax.all_to_all(send.reshape(peers, 8, tok), 'ctx', 0, 0)  10.3 us
    all_to_all x1, waiting for transfers between devices, local(): seen = lax.all_to_all(send.reshape(peers, 8, tok), 'ctx', 0, 0)  8.12 us
    pallas_call x1, Pallas kernels, local(): pl.pallas_call(weights_kernel, grid=(peers // chunk,), in_specs=[whole((c...  7.17 us
    pallas_call x1, Pallas kernels, local(): pl.pallas_call(project_kernel, grid=(depth // deep,), in_specs=[pl.BlockS...  6.21 us
  transfers between devices with their start and end apart: 2, of which 2 were waited for; matrix products, arithmetic and copies ran while one was open for 0% of the time, Pallas kernels for 7%

profile of v3, /device:TPU:1, one launch (start us, length us, event | category | flops | bytes accessed | tf_op | source)
XLA Modules:
  0.0 118.7 jit_solution(8298139227085323489)
XLA Ops:
  0.6 0.0 copy-start
  0.6 0.0 copy-start.1
  0.7 6.2 %project.1 = (bf16[192,768]{1,0:T(8,128)(2,1)S(1)}, bf16[8,2,8,768]{3,2,1,0:T(8,128)(2,1)}) custom-call(bf16[192,4096]{1,0:T(8,128)(2,1)} %bitcast.10, bf16[768,4096]{1,0:T(8,128)(2,1)} %tok_ref.3, bf16[64,768]{1,0:T(8,128)(2,1)} %cot_ref.3), custom_call_target="tpu_custom_call" | custom-call | flops 1207959552 | bytes 7864320 | tf_op jit(solution)/shard_map/project/pallas_call | solution.py:253
  6.9 0.0 copy-start.2
  6.9 10.3 %all-to-all-start = ((bf16[16,8,768]{2,1,0:T(8,128)(2,1)}), bf16[16,8,768]{2,1,0:T(8,128)(2,1)S(1)}, u32[]{:S(2)}, u32[]{:S(2)}) async-start(bf16[16,8,768]{2,1,0:T(8,128)(2,1)} %bitcast.3), calls=%async_computation | async-start | bytes 393216 | tf_op jit(solution)/shard_map/all_to_all | solution.py:285
  17.2 0.0 copy-done
  17.2 0.0 copy-done.1
  17.3 1.5 %matrices.1.rhs_ref = bf16[9,256,256]{2,1,0:T(8,128)(2,1)S(1)} custom-call(s32[1]{0:T(128)} %bitcast.group_ref, s32[24,32]{1,0:T(8,128)S(1)} %copy-done.1, bf16[24,16,256]{2,1,0:T(8,128)(2,1)S(1)} %copy-done), custom_call_target="tpu_custom_call" | custom-call | flops 5898240 | bytes 1179648 | tf_op jit(solution)/shard_map/matrices/pallas_call | solution.py:271
  18.7 8.1 %all-to-all-done.x_ref = bf16[16,8,768]{2,1,0:T(8,128)(2,1)S(1)} async-done(((bf16[16,8,768]{2,1,0:T(8,128)(2,1)}), bf16[16,8,768]{2,1,0:T(8,128)(2,1)S(1)}, u32[]{:S(2)}, u32[]{:S(2)}) %all-to-all-start) | async-done | bytes 196640 | tf_op jit(solution)/shard_map/all_to_all | solution.py:285
  26.8 0.0 copy-done.2
  26.8 5.0 %convolve.1 = bf16[16,8,896]{2,1,0:T(8,128)(2,1)S(1)} custom-call(s32[1]{0:T(128)} %bitcast.group_ref, s32[24,32]{1,0:T(8,128)S(1)} %copy-done.2, s32[24,32]{1,0:T(8,128)S(1)} %copy-done.1, bf16[16,8,768]{2,1,0:T(8,128)(2,1)S(1)} %all-to-all-done.x_ref, bf16[9,256,256]{2,1,0:T(8,128)(2,1)S(1)} %matrices.1.rhs_ref), custom_call_target="tpu_custom_call" | custom-call | flops 1811939328 | bytes 393216 | tf_op jit(solution)/shard_map/convolve/pallas_call | solution.py:286
  31.8 15.1 %all_to_all.25.back_ref = bf16[16,8,896]{2,1,0:T(8,128)(2,1)S(1)} all-to-all(bf16[16,8,896]{2,1,0:T(8,128)(2,1)S(1)} %convolve.1), channel_id=1, replica_groups=mesh['ctx'=16,'ch'=48] {'ctx'}, dimensions={0} | all-to-all | bytes 458752 | tf_op jit(solution)/shard_map/all_to_all | solution.py:309
  46.9 0.7 spread.1
  47.6 18.5 %all-to-all-start.2 = ((bf16[48,8,128]{2,1,0:T(8,128)(2,1)}), bf16[48,8,128]{2,1,0:T(8,128)(2,1)S(1)}, u32[]{:S(2)}, u32[]{:S(2)}) async-start(bf16[48,8,128]{2,1,0:T(8,128)(2,1)} %spread.1), calls=%async_computation.2 | async-start | bytes 196608 | tf_op jit(solution)/shard_map/all_to_all | solution.py:320
  66.1 7.2 %weights.1 = (bf16[64,768]{1,0:T(8,128)(2,1)}, bf16[4,864,256]{2,1,0:T(8,128)(2,1)S(1)}) custom-call(bf16[8,2,8,896]{3,2,1,0:T(8,128)(2,1)S(1)} %bitcast.9, bf16[192,768]{1,0:T(8,128)(2,1)S(1)} %get-tuple-element.10.proj_ref, bf16[64,768]{1,0:T(8,128)(2,1)} %cot_ref.3, bf16[768,4096]{1,0:T(8,128)(2,1)} %tok_ref.3), custom_call_target="tpu_custom_call" | custom-call | flops 1207959552 | bytes 9437184 | tf_op jit(solution)/shard_map/weights/pallas_call | solution.py:326
  73.3 4.9 %all-to-all-done.2.got_ref = bf16[48,8,128]{2,1,0:T(8,128)(2,1)S(1)} async-done(((bf16[48,8,128]{2,1,0:T(8,128)(2,1)}), bf16[48,8,128]{2,1,0:T(8,128)(2,1)S(1)}, u32[]{:S(2)}, u32[]{:S(2)}) %all-to-all-start.2) | async-done | bytes 98336 | tf_op jit(solution)/shard_map/all_to_all | solution.py:320
  78.2 0.1 append.1
  78.3 24.7 %all_to_all.26.got_ref = bf16[4,864,256]{2,1,0:T(8,128)(2,1)S(1)} all-to-all(bf16[4,864,256]{2,1,0:T(8,128)(2,1)S(1)} %append.1), channel_id=1, replica_groups={{0,48,96,144},{192,240,288,336},{384,432,480,528},{576,624,672,720},{1,..., dimensions={0} | all-to-all | bytes 3538944 | tf_op jit(solution)/shard_map/all_to_all | solution.py:361
  103.0 0.9 fold.1
  103.9 14.0 %all_to_all.27 = bf16[4,192,256]{2,1,0:T(8,128)(2,1)S(1)} all-to-all(bf16[4,192,256]{2,1,0:T(8,128)(2,1)S(1)} %get-tuple-element.13), channel_id=1, replica_groups={{0,192,384,576},{48,240,432,624},{96,288,480,672},{144,336,528,720},{1,..., dimensions={0} | all-to-all | bytes 786432 | tf_op jit(solution)/shard_map/all_to_all | solution.py:374
  117.9 0.7 convert_reduce_fusion
Async XLA Ops:
  0.6 16.6 %copy-start = (bf16[24,16,256]{2,1,0:T(8,128)(2,1)S(1)}, bf16[24,16,256]{2,1,0:T(8,128)(2,1)}, u32[]{:S(2)}) copy-start(bf16[24,16,256]{2,1,0:T(8,128)(2,1)} %bank_ref.1) | copy-start | bytes 589828
  0.6 16.6 %copy-start.1 = (s32[24,32]{1,0:T(8,128)S(1)}, s32[24,32]{1,0:T(8,128)}, u32[]{:S(2)}) copy-start(s32[24,32]{1,0:T(8,128)} %ids_ref.3) | copy-start | bytes 9220
  6.9 20.0 %copy-start.2 = (s32[24,32]{1,0:T(8,128)S(1)}, s32[24,32]{1,0:T(8,128)}, u32[]{:S(2)}) copy-start(s32[24,32]{1,0:T(8,128)} %lags_ref.1) | copy-start | bytes 9220
  6.9 20.0 %all-to-all-start = ((bf16[16,8,768]{2,1,0:T(8,128)(2,1)}), bf16[16,8,768]{2,1,0:T(8,128)(2,1)S(1)}, u32[]{:S(2)}, u32[]{:S(2)}) async-start(bf16[16,8,768]{2,1,0:T(8,128)(2,1)} %bitcast.3), calls=%async_computation | async-start | bytes 393216 | tf_op jit(solution)/shard_map/all_to_all | solution.py:285
  47.6 30.6 %all-to-all-start.2 = ((bf16[48,8,128]{2,1,0:T(8,128)(2,1)}), bf16[48,8,128]{2,1,0:T(8,128)(2,1)S(1)}, u32[]{:S(2)}, u32[]{:S(2)}) async-start(bf16[48,8,128]{2,1,0:T(8,128)(2,1)} %spread.1), calls=%async_computation.2 | async-start | bytes 196608 | tf_op jit(solution)/shard_map/all_to_all | solution.py:320

commit v4 on v2

--- a/solution.py
+++ b/solution.py
@@ -7,6 +7,7 @@
 
 BLK = 128
 CHUNK = 24
+LINE = 4
 HALF = 4
 BF16, F32 = jnp.bfloat16, jnp.float32
 
@@ -158,65 +159,67 @@
     total = folded[:, 0]
     for s in range(1, 8):
         total += pltpu.roll(folded[:, s], 2 * BLK - s, 1)
-    high = total.astype(BF16).astype(F32)
-    rest = total - high
     sub = lax.broadcasted_iota(jnp.int32, (8, BLK), 0)
-    for p in range(peers):
+    per_line = stored * LINE // peers
+    for y in range(peers // LINE):
         piece = jnp.zeros((8, BLK), F32)
-        for r, part in enumerate((high[:, :BLK], high[:, BLK:], rest[:, :BLK], rest[:, BLK:])):
-            piece = jnp.where(sub == r, part[p : p + 1], piece)
-        out_ref[p, :, tok:] = piece.astype(BF16)
-
-
-def weights_kernel(back_ref, proj_ref, cot_ref, tok_ref, gated_ref, out_ref, grads):
+        for r in range(2 * per_line):
+            f = y * per_line + r // 2
+            piece = jnp.where(sub == r, total[f : f + 1, (r % 2) * BLK : (r % 2 + 1) * BLK], piece)
+        for p in range(y * LINE, (y + 1) * LINE):
+            out_ref[p, :, tok:] = piece.astype(BF16)
+
+
+def grads_kernel(back_ref, proj_ref, cot_ref, gated_ref, grads):
     chan, tok = cot_ref.shape
-
-    @pl.when(pl.program_id(0) == 0)
-    def _():
-        even = back_ref[:, 0, :, :tok].astype(F32)
-        odd = back_ref[:, 1, :, :tok].astype(F32)
-        low = low_rows(even.shape)
-        conv_out = jnp.where(low, even, pltpu.roll(odd, HALF, 1)).reshape(chan, tok)
-        grad_mixed = jnp.where(low, pltpu.roll(even, HALF, 1), odd).reshape(chan, tok)
-        gated_ref[...] = (proj_ref[:chan].astype(F32) * conv_out).astype(BF16)
-        grads[:chan] = (cot_ref[...].astype(F32) * conv_out).astype(BF16)
-        grads[chan : 2 * chan] = (grad_mixed * proj_ref[2 * chan :].astype(F32)).astype(BF16)
-        grads[2 * chan :] = (grad_mixed * proj_ref[chan : 2 * chan].astype(F32)).astype(BF16)
-
-    both = jnp.dot(grads[...], tok_ref[...], preferred_element_type=F32)
-    share = out_ref.shape[2]
-    for j in range(out_ref.shape[0]):
-        out_ref[j] = both[:, j * share : (j + 1) * share].astype(out_ref.dtype)
+    even = back_ref[:, 0, :, :tok].astype(F32)
+    odd = back_ref[:, 1, :, :tok].astype(F32)
+    low = low_rows(even.shape)
+    conv_out = jnp.where(low, even, pltpu.roll(odd, HALF, 1)).reshape(chan, tok)
+    grad_mixed = jnp.where(low, pltpu.roll(even, HALF, 1), odd).reshape(chan, tok)
+    gated_ref[...] = (proj_ref[:chan].astype(F32) * conv_out).astype(BF16)
+    grads[:chan] = (cot_ref[...].astype(F32) * conv_out).astype(BF16)
+    grads[chan : 2 * chan] = (grad_mixed * proj_ref[2 * chan :].astype(F32)).astype(BF16)
+    grads[2 * chan :] = (grad_mixed * proj_ref[chan : 2 * chan].astype(F32)).astype(BF16)
+
+
+def weights_kernel(_, grads_ref, tok_ref, out_ref):
+    out_ref[0] = jnp.dot(grads_ref[...], tok_ref[...], preferred_element_type=F32).astype(BF16)
 
 
 def spread_kernel(back_ref, out_ref):
     both = jnp.sum(back_ref[...].astype(F32), axis=0)
-    both += pltpu.roll(both, 6, 0)
-    high = both.astype(BF16).astype(F32)
-    sub = lax.broadcasted_iota(jnp.int32, both.shape, 0)
-    piece = jnp.where(sub < 2, high, jnp.where(sub < 4, pltpu.roll(both - high, 2, 0), 0.0))
-    out_ref[...] = jnp.broadcast_to(piece.astype(BF16)[None], out_ref.shape)
-
-
-def append_kernel(got_ref, _, out_ref, held):
+    out_ref[...] = jnp.broadcast_to(both.astype(BF16)[None], out_ref.shape)
+
+
+def fold_kernel(own_ref, a_ref, b_ref, c_ref, got_ref, out_ref, held):
+    lines, rows = own_ref.shape[:2]
+    for y in range(lines):
+        total = own_ref[y].astype(F32) + a_ref[y].astype(F32)
+        total += b_ref[y].astype(F32) + c_ref[y].astype(F32)
+        out_ref[y, :rows] = total.astype(BF16)
     groups = held.shape[0]
     both = got_ref[...].astype(F32)
-    both += pltpu.roll(both, 6, 1)
     held[...] = jnp.sum(both.reshape(groups, -1, *both.shape[1:]), axis=1)
-    rows = jnp.concatenate([held[:, 0], held[:, 1]], axis=1).astype(BF16)
-    if out_ref.shape[1] > groups:
-        rows = jnp.concatenate([rows, jnp.zeros((out_ref.shape[1] - groups, rows.shape[1]), BF16)], 0)
-    out_ref[...] = jnp.broadcast_to(rows[None], out_ref.shape)
+    per_line = held.shape[1] // 2
+    for j in range(per_line):
+        part = jnp.concatenate([held[:, 2 * j], held[:, 2 * j + 1]], axis=1).astype(BF16)
+        start = rows + j * groups
+        for y in range(lines):
+            out_ref[y, start : start + groups] = part
 
 
 def finish_kernel(got_ref, w_ref, table_ref):
     rows = w_ref.shape[0]
     total = got_ref[0, :rows].astype(F32)
-    for p in range(1, got_ref.shape[0]):
-        total += got_ref[p, :rows].astype(F32)
+    for y in range(1, got_ref.shape[0]):
+        total += got_ref[y, :rows].astype(F32)
     w_ref[...] = total
-    for p in range(got_ref.shape[0]):
-        table_ref[:, p] = got_ref[p, rows : rows + table_ref.shape[0]].astype(F32)
+    groups, stored = table_ref.shape[:2]
+    per_line = stored // got_ref.shape[0]
+    for f in range(stored):
+        start = rows + (f % per_line) * groups
+        table_ref[:, f] = got_ref[f // per_line, start : start + groups].astype(F32)
 
 
 def whole(shape):
@@ -304,66 +307,86 @@
         name="convolve",
     )(group, lag_blocks, filter_ids, seen, rhs)
     got = lax.all_to_all(back, "ctx", 0, 0)
-    lines = lax.axis_size("ch")
+    wide = lax.axis_size("ch")
     piece = pl.pallas_call(
         spread_kernel,
         grid=(1,),
         in_specs=[pl.BlockSpec((peers, 8, BLK), lambda i: (0, 0, tok // BLK))],
-        out_specs=whole((lines, 8, BLK)),
-        out_shape=jax.ShapeDtypeStruct((lines, 8, BLK), BF16),
+        out_specs=whole((wide, 8, BLK)),
+        out_shape=jax.ShapeDtypeStruct((wide, 8, BLK), BF16),
         compiler_params=params(4),
         name="spread",
     )(got)
     tables = lax.all_to_all(piece, "ch", 0, 0)
-    chunk = 2
     rows = 3 * chan
-    lines_in = -(-groups // 8) * 8
-    gated, partial = pl.pallas_call(
-        weights_kernel,
-        grid=(peers // chunk,),
-        in_specs=[
-            whole((chan // 8, 2, 8, tok + BLK)),
-            whole((rows, tok)),
-            whole((chan, tok)),
-            pl.BlockSpec((tok, chunk * share), lambda i: (0, i)),
-        ],
-        out_specs=[
-            whole((chan, tok)),
-            pl.BlockSpec((chunk, rows, share), lambda i: (i, 0, 0)),
-        ],
+    lines = peers // LINE
+    gated, grads = pl.pallas_call(
+        grads_kernel,
+        grid=(1,),
+        in_specs=[whole((chan // 8, 2, 8, tok + BLK)), whole((rows, tok)), whole((chan, tok))],
+        out_specs=[whole((chan, tok)), whole((rows, tok))],
         out_shape=[
             jax.ShapeDtypeStruct((chan, tok), BF16),
-            jax.ShapeDtypeStruct((peers, rows + lines_in, share), BF16),
+            jax.ShapeDtypeStruct((rows, tok), BF16),
         ],
-        scratch_shapes=[pltpu.VMEM((rows, tok), BF16)],
-        compiler_params=params(20),
-        cost_estimate=cost(6 * chan * depth * tok, 2 * depth * (tok + 6 * chan)),
-        name="weights",
-    )(got.reshape(chan // 8, 2, 8, tok + BLK), proj, grad_out, tokens_in)
-    partial = pl.pallas_call(
-        append_kernel,
+        compiler_params=params(8),
+        cost_estimate=cost(8 * rows * tok, 8 * rows * tok),
+        name="grads",
+    )(got.reshape(chan // 8, 2, 8, tok + BLK), proj, grad_out)
+    place = lax.rem(lax.axis_index("ctx"), LINE)
+
+    def part(offset):
+        dest = lax.rem(place + offset, LINE).astype(jnp.int32)[None]
+        return pl.pallas_call(
+            weights_kernel,
+            grid_spec=pltpu.PrefetchScalarGridSpec(
+                num_scalar_prefetch=1,
+                grid=(lines,),
+                in_specs=[
+                    whole((rows, tok)),
+                    pl.BlockSpec((tok, share), lambda i, x: (0, i * LINE + x[0])),
+                ],
+                out_specs=pl.BlockSpec((1, rows, share), lambda i, x: (i, 0, 0)),
+            ),
+            out_shape=jax.ShapeDtypeStruct((lines, rows, share), BF16),
+            compiler_params=params(8),
+            cost_estimate=cost(2 * rows * lines * share * tok, 2 * lines * share * (tok + rows)),
+            name="weights",
+        )(dest, grads, tokens_in)
+
+    def sent(offset):
+        pairs_of = [
+            (c, c // LINE * LINE + (c % LINE + offset) % LINE) for c in range(peers)
+        ]
+        return lax.ppermute(part(offset), "ctx", pairs_of)
+
+    others = [sent(offset) for offset in (2, 1, 3)]
+    own = part(0)
+    extra = groups * (stored // lines)
+    folded = pl.pallas_call(
+        fold_kernel,
         grid=(1,),
-        in_specs=[whole((lines, 8, BLK)), pl.BlockSpec(memory_space=pl.ANY)],
-        out_specs=pl.BlockSpec((peers, lines_in, share), lambda i: (0, rows // lines_in, 0)),
-        out_shape=jax.ShapeDtypeStruct(partial.shape, BF16),
+        in_specs=[whole(own.shape)] * 4 + [whole(tables.shape)],
+        out_specs=whole((lines, rows + extra, share)),
+        out_shape=jax.ShapeDtypeStruct((lines, rows + extra, share), BF16),
         scratch_shapes=[pltpu.VMEM((groups, 8, BLK), F32)],
-        input_output_aliases={1: 0},
-        compiler_params=params(8),
-        name="append",
-    )(tables, partial)
-    parts = lax.all_to_all(partial, "ctx", 0, 0)
+        compiler_params=params(12),
+        name="fold",
+    )(own, *others, tables)
+    along_y = [[y * LINE + x for y in range(lines)] for x in range(LINE)]
+    sums = lax.all_to_all(folded, "ctx", 0, 0, axis_index_groups=along_y)
     w_grad, filter_grad = pl.pallas_call(
         finish_kernel,
         grid=(1,),
-        in_specs=[whole(parts.shape)],
-        out_specs=[whole((rows, share)), whole((groups, peers, share))],
+        in_specs=[whole(sums.shape)],
+        out_specs=[whole((rows, share)), whole((groups, stored, share))],
         out_shape=[
             jax.ShapeDtypeStruct((rows, share), F32),
-            jax.ShapeDtypeStruct((groups, peers, share), F32),
+            jax.ShapeDtypeStruct((groups, stored, share), F32),
         ],
-        compiler_params=params(10),
+        compiler_params=params(8),
         name="finish",
-    )(parts)
+    )(sums)
     w_grad = jnp.transpose(w_grad.reshape(3, chan, share), (2, 0, 1))
     return gated, w_grad, filter_grad
 

time: 127 us -> 121 us (0.953)
  blocking collectives: 62 us -> 19.3 us
  starting transfers between devices: 28.8 us -> 44.8 us
  waiting for transfers between devices: 13.2 us -> 27.2 us
  Pallas kernels: 21.5 us -> 27.9 us
    all_to_all x2 -> x1, blocking collectives: 62 us -> 19.3 us  [local(): sums = lax.all_to_all(folded, 'ctx', 0, 0, axis_index_groups=along_y)]
    ppermute x0 -> x3, starting transfers between devices: none -> 10.3 us  [sent(): return lax.ppermute(part(offset), 'ctx', pairs_of)]
    all_to_all x0 -> x1, waiting for transfers between devices: none -> 9.84 us  [local(): got = lax.all_to_all(back, 'ctx', 0, 0)]
    pallas_call x3 -> x7, Pallas kernels: 8.18 us -> 14.1 us  [the longest x4 11.2 us: part(): pl.pallas_call(weights_kernel, grid_spec=pltpu.PrefetchScalarGridSpec(num...]
    all_to_all x0 -> x1, starting transfers between devices: none -> 5.45 us  [local(): got = lax.all_to_all(back, 'ctx', 0, 0)]
    all_to_all x1, waiting for transfers between devices: 5.06 us -> 9.22 us  [local(): tables = lax.all_to_all(piece, 'ch', 0, 0)]
  transfers between devices with their start and end apart: 2 -> 6, of which waited for: 2 -> 3; matrix products, arithmetic and copies ran while one was open for 0% -> 0% of each run, Pallas kernels for 7% -> 4%
where the time goes in v4:
time: 121 us; the launch traced here: 120 us
  starting transfers between devices  44.8 us (37%)
  Pallas kernels  27.9 us (23%)
  waiting for transfers between devices  27.2 us (22%)
  blocking collectives  19.3 us (16%)
    all_to_all x1, blocking collectives, local(): sums = lax.all_to_all(folded, 'ctx', 0, 0, axis_index_groups=along_y)  19.3 us
    all_to_all x1, starting transfers between devices, local(): tables = lax.all_to_all(piece, 'ch', 0, 0)  18.8 us
    pallas_call x4, Pallas kernels, part(): pl.pallas_call(weights_kernel, grid_spec=pltpu.PrefetchScalarGridSpec(num...  11.2 us
    all_to_all x1, starting transfers between devices, local(): seen = lax.all_to_all(send.reshape(peers, 8, tok), 'ctx', 0, 0)  10.3 us
    ppermute x3, starting transfers between devices, sent(): return lax.ppermute(part(offset), 'ctx', pairs_of)  10.3 us
    all_to_all x1, waiting for transfers between devices, local(): got = lax.all_to_all(back, 'ctx', 0, 0)  9.84 us
    all_to_all x1, waiting for transfers between devices, local(): tables = lax.all_to_all(piece, 'ch', 0, 0)  9.22 us
    all_to_all x1, waiting for transfers between devices, local(): seen = lax.all_to_all(send.reshape(peers, 8, tok), 'ctx', 0, 0)  8.12 us
  transfers between devices with their start and end apart: 6, of which 3 were waited for; matrix products, arithmetic and copies ran while one was open for 0% of the time, Pallas kernels for 4%

profile of v4, /device:TPU:1, one launch (start us, length us, event | category | flops | bytes accessed | tf_op | source)
XLA Modules:
  0.0 120.0 jit_solution(16560925463388401015)
XLA Ops:
  0.6 0.0 copy-start
  0.6 0.0 copy-start.1
  0.7 6.2 %project.1 = (bf16[192,768]{1,0:T(8,128)(2,1)S(1)}, bf16[8,2,8,768]{3,2,1,0:T(8,128)(2,1)}) custom-call(bf16[192,4096]{1,0:T(8,128)(2,1)} %bitcast.14, bf16[768,4096]{1,0:T(8,128)(2,1)} %tok_ref.9, bf16[64,768]{1,0:T(8,128)(2,1)} %cot_ref.3), custom_call_target="tpu_custom_call" | custom-call | flops 1207959552 | bytes 7864320 | tf_op jit(solution)/shard_map/project/pallas_call | solution.py:253
  6.9 0.0 copy-start.2
  6.9 10.3 %all-to-all-start = ((bf16[16,8,768]{2,1,0:T(8,128)(2,1)}), bf16[16,8,768]{2,1,0:T(8,128)(2,1)S(1)}, u32[]{:S(2)}, u32[]{:S(2)}) async-start(bf16[16,8,768]{2,1,0:T(8,128)(2,1)} %bitcast.3), calls=%async_computation | async-start | bytes 393216 | tf_op jit(solution)/shard_map/all_to_all | solution.py:285
  17.2 0.0 copy-done
  17.2 0.0 copy-done.1
  17.3 1.5 %matrices.1.rhs_ref = bf16[9,256,256]{2,1,0:T(8,128)(2,1)S(1)} custom-call(s32[1]{0:T(128)} %bitcast.group_ref, s32[24,32]{1,0:T(8,128)S(1)} %copy-done.1, bf16[24,16,256]{2,1,0:T(8,128)(2,1)S(1)} %copy-done), custom_call_target="tpu_custom_call" | custom-call | flops 5898240 | bytes 1179648 | tf_op jit(solution)/shard_map/matrices/pallas_call | solution.py:271
  18.7 8.1 %all-to-all-done.x_ref = bf16[16,8,768]{2,1,0:T(8,128)(2,1)S(1)} async-done(((bf16[16,8,768]{2,1,0:T(8,128)(2,1)}), bf16[16,8,768]{2,1,0:T(8,128)(2,1)S(1)}, u32[]{:S(2)}, u32[]{:S(2)}) %all-to-all-start) | async-done | bytes 196640 | tf_op jit(solution)/shard_map/all_to_all | solution.py:285
  26.8 0.0 copy-done.2
  26.8 5.4 %convolve.1 = bf16[16,8,896]{2,1,0:T(8,128)(2,1)} custom-call(s32[1]{0:T(128)} %bitcast.group_ref, s32[24,32]{1,0:T(8,128)S(1)} %copy-done.2, s32[24,32]{1,0:T(8,128)S(1)} %copy-done.1, bf16[16,8,768]{2,1,0:T(8,128)(2,1)S(1)} %all-to-all-done.x_ref, bf16[9,256,256]{2,1,0:T(8,128)(2,1)S(1)} %matrices.1.rhs_ref), custom_call_target="tpu_custom_call" | custom-call | flops 1811939328 | bytes 393216 | tf_op jit(solution)/shard_map/convolve/pallas_call | solution.py:286
  32.2 5.5 %all-to-all-start.1 = ((bf16[16,8,896]{2,1,0:T(8,128)(2,1)}), bf16[16,8,896]{2,1,0:T(8,128)(2,1)S(1)}, u32[]{:S(2)}, u32[]{:S(2)}) async-start(bf16[16,8,896]{2,1,0:T(8,128)(2,1)} %convolve.1), calls=%async_computation.1 | async-start | bytes 458752 | tf_op jit(solution)/shard_map/all_to_all | solution.py:309
  37.7 9.8 %all-to-all-done.1.back_ref = bf16[16,8,896]{2,1,0:T(8,128)(2,1)S(1)} async-done(((bf16[16,8,896]{2,1,0:T(8,128)(2,1)}), bf16[16,8,896]{2,1,0:T(8,128)(2,1)S(1)}, u32[]{:S(2)}, u32[]{:S(2)}) %all-to-all-start.1) | async-done | bytes 229408 | tf_op jit(solution)/shard_map/all_to_all | solution.py:309
  47.6 1.6 %grads.1 = (bf16[64,768]{1,0:T(8,128)(2,1)}, bf16[192,768]{1,0:T(8,128)(2,1)S(1)}) custom-call(bf16[8,2,8,896]{3,2,1,0:T(8,128)(2,1)S(1)} %bitcast.13, bf16[192,768]{1,0:T(8,128)(2,1)S(1)} %get-tuple-element.10.proj_ref, bf16[64,768]{1,0:T(8,128)(2,1)} %cot_ref.3), custom_call_target="tpu_custom_call" | custom-call | flops 1179648 | bytes 1179648 | tf_op jit(solution)/shard_map/grads/pallas_call | solution.py:323
  49.2 2.8 %weights.7 = bf16[4,192,256]{2,1,0:T(8,128)(2,1)S(1)} custom-call(s32[1]{0:T(128)} %bitcast.8._, bf16[192,768]{1,0:T(8,128)(2,1)S(1)} %get-tuple-element.12.grads_ref, bf16[768,4096]{1,0:T(8,128)(2,1)} %tok_ref.9), custom_call_target="tpu_custom_call" | custom-call | flops 301989888 | bytes 1966080 | tf_op jit(solution)/shard_map/weights/pallas_call | solution.py:340
  52.0 2.8 %weights.6 = bf16[4,192,256]{2,1,0:T(8,128)(2,1)S(1)} custom-call(s32[1]{0:T(128)} %bitcast.7._, bf16[192,768]{1,0:T(8,128)(2,1)S(1)} %get-tuple-element.12.grads_ref, bf16[768,4096]{1,0:T(8,128)(2,1)} %tok_ref.9), custom_call_target="tpu_custom_call" | custom-call | flops 301989888 | bytes 1966080 | tf_op jit(solution)/shard_map/weights/pallas_call | solution.py:340
  54.8 2.8 %weights.5 = bf16[4,192,256]{2,1,0:T(8,128)(2,1)S(1)} custom-call(s32[1]{0:T(128)} %bitcast.6._, bf16[192,768]{1,0:T(8,128)(2,1)S(1)} %get-tuple-element.12.grads_ref, bf16[768,4096]{1,0:T(8,128)(2,1)} %tok_ref.9), custom_call_target="tpu_custom_call" | custom-call | flops 301989888 | bytes 1966080 | tf_op jit(solution)/shard_map/weights/pallas_call | solution.py:340
  57.6 3.8 %collective-permute-start = (bf16[4,192,256]{2,1,0:T(8,128)(2,1)S(1)}, bf16[4,192,256]{2,1,0:T(8,128)(2,1)S(1)}, u32[]{:S(2)}, u32[]{:S(2)}) collective-permute-start(bf16[4,192,256]{2,1,0:T(8,128)(2,1)S(1)} %weights.5), channel_id=1, source_target_pairs={{0,96},{48,144},{96,0},{144,48},{192,288},{240,336},{288,192},{336... | collective-permute-start | bytes 1179656 | tf_op jit(solution)/shard_map/ppermute | solution.py:361
  61.4 1.9 %collective-permute-start.1 = (bf16[4,192,256]{2,1,0:T(8,128)(2,1)S(1)}, bf16[4,192,256]{2,1,0:T(8,128)(2,1)S(1)}, u32[]{:S(2)}, u32[]{:S(2)}) collective-permute-start(bf16[4,192,256]{2,1,0:T(8,128)(2,1)S(1)} %weights.6), channel_id=1, source_target_pairs={{0,48},{48,96},{96,144},{144,0},{192,240},{240,288},{288,336},{336... | collective-permute-start | bytes 1179656 | tf_op jit(solution)/shard_map/ppermute | solution.py:361
  63.3 4.6 %collective-permute-start.2 = (bf16[4,192,256]{2,1,0:T(8,128)(2,1)S(1)}, bf16[4,192,256]{2,1,0:T(8,128)(2,1)S(1)}, u32[]{:S(2)}, u32[]{:S(2)}) collective-permute-start(bf16[4,192,256]{2,1,0:T(8,128)(2,1)S(1)} %weights.7), channel_id=1, source_target_pairs={{0,144},{48,0},{96,48},{144,96},{192,336},{240,192},{288,240},{336... | collective-permute-start | bytes 1179656 | tf_op jit(solution)/shard_map/ppermute | solution.py:361
  67.9 0.7 spread.1
  68.6 18.8 %all-to-all-start.2 = ((bf16[48,8,128]{2,1,0:T(8,128)(2,1)}), bf16[48,8,128]{2,1,0:T(8,128)(2,1)S(1)}, u32[]{:S(2)}, u32[]{:S(2)}) async-start(bf16[48,8,128]{2,1,0:T(8,128)(2,1)} %spread.1), calls=%async_computation.2 | async-start | bytes 196608 | tf_op jit(solution)/shard_map/all_to_all | solution.py:320
  87.4 2.8 %weights.4.own_ref = bf16[4,192,256]{2,1,0:T(8,128)(2,1)S(1)} custom-call(s32[1]{0:T(128)} %bitcast.5._, bf16[192,768]{1,0:T(8,128)(2,1)S(1)} %get-tuple-element.12.grads_ref, bf16[768,4096]{1,0:T(8,128)(2,1)} %tok_ref.9), custom_call_target="tpu_custom_call" | custom-call | flops 301989888 | bytes 1966080 | tf_op jit(solution)/shard_map/weights/pallas_call | solution.py:340
  90.2 9.2 %all-to-all-done.2.got_ref = bf16[48,8,128]{2,1,0:T(8,128)(2,1)S(1)} async-done(((bf16[48,8,128]{2,1,0:T(8,128)(2,1)}), bf16[48,8,128]{2,1,0:T(8,128)(2,1)S(1)}, u32[]{:S(2)}, u32[]{:S(2)}) %all-to-all-start.2) | async-done | bytes 98336 | tf_op jit(solution)/shard_map/all_to_all | solution.py:320
  99.4 0.0 collective-permute-done.a_ref
  99.4 0.0 collective-permute-done.1.b_ref
  99.4 0.0 collective-permute-done.2.c_ref
  99.4 0.3 fold.1
  99.8 19.3 %all_to_all.20.got_ref = bf16[4,288,256]{2,1,0:T(8,128)(2,1)S(1)} all-to-all(bf16[4,288,256]{2,1,0:T(8,128)(2,1)S(1)} %fold.1), channel_id=1, replica_groups={{0,192,384,576},{48,240,432,624},{96,288,480,672},{144,336,528,720},{1,..., dimensions={0} | all-to-all | bytes 1179648 | tf_op jit(solution)/shard_map/all_to_all | solution.py:377
  119.0 1.0 finish.1
Async XLA Ops:
  0.6 16.6 %copy-start = (bf16[24,16,256]{2,1,0:T(8,128)(2,1)S(1)}, bf16[24,16,256]{2,1,0:T(8,128)(2,1)}, u32[]{:S(2)}) copy-start(bf16[24,16,256]{2,1,0:T(8,128)(2,1)} %bank_ref.1) | copy-start | bytes 589828
  0.6 16.6 %copy-start.1 = (s32[24,32]{1,0:T(8,128)S(1)}, s32[24,32]{1,0:T(8,128)}, u32[]{:S(2)}) copy-start(s32[24,32]{1,0:T(8,128)} %ids_ref.3) | copy-start | bytes 9220
  6.9 20.0 %copy-start.2 = (s32[24,32]{1,0:T(8,128)S(1)}, s32[24,32]{1,0:T(8,128)}, u32[]{:S(2)}) copy-start(s32[24,32]{1,0:T(8,128)} %lags_ref.1) | copy-start | bytes 9220
  6.9 20.0 %all-to-all-start = ((bf16[16,8,768]{2,1,0:T(8,128)(2,1)}), bf16[16,8,768]{2,1,0:T(8,128)(2,1)S(1)}, u32[]{:S(2)}, u32[]{:S(2)}) async-start(bf16[16,8,768]{2,1,0:T(8,128)(2,1)} %bitcast.3), calls=%async_computation | async-start | bytes 393216 | tf_op jit(solution)/shard_map/all_to_all | solution.py:285
  32.2 15.3 %all-to-all-start.1 = ((bf16[16,8,896]{2,1,0:T(8,128)(2,1)}), bf16[16,8,896]{2,1,0:T(8,128)(2,1)S(1)}, u32[]{:S(2)}, u32[]{:S(2)}) async-start(bf16[16,8,896]{2,1,0:T(8,128)(2,1)} %convolve.1), calls=%async_computation.1 | async-start | bytes 458752 | tf_op jit(solution)/shard_map/all_to_all | solution.py:309
  57.6 41.8 %collective-permute-start = (bf16[4,192,256]{2,1,0:T(8,128)(2,1)S(1)}, bf16[4,192,256]{2,1,0:T(8,128)(2,1)S(1)}, u32[]{:S(2)}, u32[]{:S(2)}) collective-permute-start(bf16[4,192,256]{2,1,0:T(8,128)(2,1)S(1)} %weights.5), channel_id=1, source_target_pairs={{0,96},{48,144},{96,0},{144,48},{192,288},{240,336},{288,192},{336... | collective-permute-start | bytes 1179656 | tf_op jit(solution)/shard_map/ppermute | solution.py:361
  61.4 38.0 %collective-permute-start.1 = (bf16[4,192,256]{2,1,0:T(8,128)(2,1)S(1)}, bf16[4,192,256]{2,1,0:T(8,128)(2,1)S(1)}, u32[]{:S(2)}, u32[]{:S(2)}) collective-permute-start(bf16[4,192,256]{2,1,0:T(8,128)(2,1)S(1)} %weights.6), channel_id=1, source_target_pairs={{0,48},{48,96},{96,144},{144,0},{192,240},{240,288},{288,336},{336... | collective-permute-start | bytes 1179656 | tf_op jit(solution)/shard_map/ppermute | solution.py:361
  63.3 36.1 %collective-permute-start.2 = (bf16[4,192,256]{2,1,0:T(8,128)(2,1)S(1)}, bf16[4,192,256]{2,1,0:T(8,128)(2,1)S(1)}, u32[]{:S(2)}, u32[]{:S(2)}) collective-permute-start(bf16[4,192,256]{2,1,0:T(8,128)(2,1)S(1)} %weights.7), channel_id=1, source_target_pairs={{0,144},{48,0},{96,48},{144,96},{192,336},{240,192},{288,240},{336... | collective-permute-start | bytes 1179656 | tf_op jit(solution)/shard_map/ppermute | solution.py:361
  68.6 30.8 %all-to-all-start.2 = ((bf16[48,8,128]{2,1,0:T(8,128)(2,1)}), bf16[48,8,128]{2,1,0:T(8,128)(2,1)S(1)}, u32[]{:S(2)}, u32[]{:S(2)}) async-start(bf16[48,8,128]{2,1,0:T(8,128)(2,1)} %spread.1), calls=%async_computation.2 | async-start | bytes 196608 | tf_op jit(solution)/shard_map/all_to_all | solution.py:320
